TPU v7x, 512 devices: a whole 4x4x16 slice. The times are simulated.
512 devices in a mesh: dp: 16 (over x, z_lo), expert: 32 (over y, z_hi, core).
Axes of the slice: x: 4, y: 4, z: 16 (z_hi: 4, z_lo: 4; z = z_hi * 4 + z_lo), core: 2. Of those that a mesh axis runs over, the one named last changes fastest.
Arguments:
- tokens: bfloat16 [4096, 2560], P(('dp', 'expert')), may hold values from -24 to 24
- routes: int32 [4096, 6], P(('dp', 'expert')), may hold values from 0 to 7, all different within a row; in each aligned block of 8 rows (0 to 7, 8 to 15, ...) at most 7 rows name the same one
- router: float32 [2560, 8], replicated, may hold values from -0.125 to 0.125
- w_gate: bfloat16 [2560, 8192], P(None, 'expert'), may hold values from -0.125 to 0.125
- w_up: bfloat16 [2560, 8192], P(None, 'expert'), may hold values from -0.125 to 0.125
- w_down: bfloat16 [2560, 8192], P(None, 'expert'), may hold values from -0.1875 to 0.1875
- cotangent: bfloat16 [4096, 2560], P(('dp', 'expert')), may hold values from -6 to 6
Outputs:
- mixed: bfloat16 [4096, 2560], P(('dp', 'expert'))
- grad_tokens: bfloat16 [4096, 2560], P(('dp', 'expert'))
- grad_router: float32 [2560, 8], replicated
- grad_gate: float32 [2560, 8192], P('dp', 'expert')
- grad_up: float32 [2560, 8192], P('dp', 'expert')
- grad_down: float32 [2560, 8192], P('dp', 'expert')
Inputs may be any that keep to these rules, and one draw needn't show every extreme that they name: `routes`: each row names 6 different experts. Among the rows of one device no expert is named more than 7 times, and in every draw some expert is named exactly 7 times by the rows of some device.
All inputs are finite; a program needn't handle non-finite values.
Results may differ from a plain program's by a relative error of at most 0.02.
Values may be sent and summed in bfloat16 or wider, within the bound.
A program may use at most 64 MiB of HBM per device.

v0:
```python
import jax
import jax.numpy as jnp
from jax import lax
from jax.sharding import PartitionSpec as P


def expert_hidden(inputs, gate_matrix, up_matrix):
    gate_pre = jnp.dot(inputs, gate_matrix, preferred_element_type=jnp.float32)
    up_pre = jnp.dot(inputs, up_matrix, preferred_element_type=jnp.float32)
    hidden = (jax.nn.silu(gate_pre) * up_pre).astype(jnp.bfloat16)
    return (gate_pre, up_pre, hidden)


def expert_backward(slot_grad, gate_pre, up_pre, gate_matrix, up_matrix, down_matrix):
    hidden_grad = jnp.dot(slot_grad, down_matrix, preferred_element_type=jnp.float32)
    sigma = jax.nn.sigmoid(gate_pre)
    gate_grad = (hidden_grad * up_pre * sigma * (1.0 + gate_pre * (1.0 - sigma))).astype(
        jnp.bfloat16
    )
    up_grad = (hidden_grad * gate_pre * sigma).astype(jnp.bfloat16)
    contract = (((1,), (1,)), ((), ()))
    input_grad = lax.dot_general(
        gate_grad, gate_matrix, contract, preferred_element_type=jnp.float32
    )
    input_grad = input_grad + lax.dot_general(
        up_grad, up_matrix, contract, preferred_element_type=jnp.float32
    )
    return (gate_grad, up_grad, input_grad.astype(jnp.bfloat16))


def return_grads(input_part):
    return lax.all_to_all(input_part, "expert", split_axis=0, concat_axis=0, tiled=True)


def local(tokens, routes, router, w_gate, w_up, w_down, cotangent):
    features = tokens.shape[1]
    experts = router.shape[1]
    fanout = routes.shape[1]
    tok_count = tokens.shape[0]
    hidden_units = w_gate.shape[1]
    sharing = lax.axis_size("expert") // experts
    capacity = min(tok_count, 5 * fanout * tok_count // (4 * experts))
    highest = lax.Precision.HIGHEST
    tokens_wide = tokens.astype(jnp.float32)
    logits = jnp.dot(tokens_wide, router, precision=highest)
    expert_ids = jnp.arange(experts, dtype=jnp.int32)
    choose = routes[:, :, None] == expert_ids[None, None, :]
    choose_f = choose.astype(jnp.float32)
    picked = jnp.sum(choose_f * logits[:, None, :], axis=2)
    affinity = jax.nn.sigmoid(picked)
    denominator = jnp.sum(affinity, axis=1, keepdims=True)
    gate_values = affinity / denominator
    choose_i = choose.astype(jnp.int32)
    per_token = jnp.sum(choose_i, axis=1)
    before = jnp.cumsum(per_token, axis=0) - per_token
    position = jnp.sum(choose_i * before[:, None, :], axis=2)
    slot_ids = jnp.arange(capacity, dtype=jnp.int32)
    placed = choose_f[:, :, :, None] * (
        position[:, :, None, None] == slot_ids[None, None, None, :]
    ).astype(jnp.float32)
    slot_table = jnp.sum(placed, axis=1)
    gate_table = jnp.einsum("tkec,tk->tec", placed, gate_values)
    table_narrow = slot_table.astype(jnp.bfloat16)
    outgoing = jnp.einsum(
        "tec,td->ecd", table_narrow, tokens, preferred_element_type=jnp.float32
    ).astype(jnp.bfloat16)
    outgoing_all = jnp.repeat(outgoing, sharing, axis=0)

    def merge_parts(parts):
        wide_parts = parts.astype(jnp.float32)
        return jnp.sum(wide_parts.reshape(experts, sharing, capacity, features), axis=1)

    received = lax.all_to_all(outgoing_all, "expert", split_axis=0, concat_axis=0, tiled=True)
    sources, item_count, _ = received.shape
    expert_rows = received.reshape(sources * item_count, features)
    gate_pre, up_pre, hidden = expert_hidden(expert_rows, w_gate, w_up)
    output = lax.dot_general(
        hidden, w_down, (((1,), (1,)), ((), ())), preferred_element_type=jnp.float32
    )
    output = output.astype(jnp.bfloat16).reshape(sources, item_count, features)
    returned = lax.all_to_all(output, "expert", split_axis=0, concat_axis=0, tiled=True)
    returned, rows_kept, gate_kept, up_kept, hidden_kept = (
        returned,
        received,
        gate_pre.reshape(sources, item_count, hidden_units),
        up_pre.reshape(sources, item_count, hidden_units),
        hidden.reshape(sources, item_count, hidden_units),
    )
    expert_out = merge_parts(returned).astype(jnp.bfloat16)
    expert_wide = lax.optimization_barrier(expert_out).astype(jnp.float32)
    mixed = jnp.einsum("tec,ecd->td", gate_table, expert_wide).astype(jnp.bfloat16)
    grad_slots = jnp.einsum(
        "tec,td->ecd", table_narrow, cotangent, preferred_element_type=jnp.float32
    ).astype(jnp.bfloat16)
    slot_pull = jnp.sum(grad_slots.astype(jnp.float32) * expert_wide, axis=2)
    expert_pull = jnp.einsum("tec,ec->te", slot_table, slot_pull)
    gate_pull = jnp.sum(choose_f * expert_pull[:, None, :], axis=2)
    mean_pull = jnp.sum(gate_values * gate_pull, axis=1, keepdims=True)
    logit_grad = (gate_pull - mean_pull) / denominator * affinity * (1.0 - affinity)
    per_logit = jnp.sum(choose_f * logit_grad[:, :, None], axis=1)
    router_part = jnp.dot(tokens_wide.T, per_logit, precision=highest)
    grad_router = lax.psum(router_part, ("dp", "expert"))
    slot_gate = jnp.sum(gate_table, axis=0)
    grad_outgoing = (slot_gate[:, :, None] * grad_slots.astype(jnp.float32)).astype(jnp.bfloat16)
    grad_outgoing_all = jnp.repeat(grad_outgoing, sharing, axis=0)
    row_items = lax.all_to_all(outgoing_all, "expert", split_axis=0, concat_axis=0, tiled=True)
    grad_items = lax.all_to_all(
        grad_outgoing_all, "expert", split_axis=0, concat_axis=0, tiled=True
    )
    sources, item_count, _ = row_items.shape
    expert_rows = row_items.reshape(-1, features)
    grad_rows = grad_items.reshape(-1, features)
    gate_pre, up_pre, hidden = expert_hidden(expert_rows, w_gate, w_up)
    backward_gate_grad, backward_up_grad, input_part = expert_backward(
        grad_rows, gate_pre, up_pre, w_gate, w_up, w_down
    )
    input_back = return_grads(input_part.reshape(sources, item_count, features))
    input_back, rows_again, grads_again, hidden_again, gate_again, up_again = (
        input_back,
        row_items,
        grad_items,
        hidden.reshape(sources, item_count, hidden_units),
        backward_gate_grad.reshape(sources, item_count, hidden_units),
        backward_up_grad.reshape(sources, item_count, hidden_units),
    )
    rows_flat = rows_again.reshape(-1, features)
    grad_flat = grads_again.reshape(-1, features)
    hidden_flat = hidden_again.reshape(-1, hidden_units)
    gate_grad = gate_again.reshape(-1, hidden_units)
    up_grad = up_again.reshape(-1, hidden_units)
    contract = (((0,), (0,)), ((), ()))
    part_gate = lax.dot_general(rows_flat, gate_grad, contract, preferred_element_type=jnp.float32)
    part_up = lax.dot_general(rows_flat, up_grad, contract, preferred_element_type=jnp.float32)
    part_down = lax.dot_general(
        grad_flat, hidden_flat, contract, preferred_element_type=jnp.float32
    )
    summed = lax.psum_scatter(
        jnp.concatenate([part_gate, part_up, part_down], axis=1).astype(jnp.bfloat16),
        "dp",
        scatter_dimension=0,
        tiled=True,
    ).astype(jnp.float32)
    grad_gate = summed[:, :hidden_units]
    grad_up = summed[:, hidden_units : 2 * hidden_units]
    grad_down = summed[:, 2 * hidden_units :]
    input_grad = merge_parts(input_back).astype(jnp.bfloat16)
    input_wide = lax.optimization_barrier(input_grad).astype(jnp.float32)
    router_back = lax.dot_general(per_logit, router, (((1,), (1,)), ((), ())), precision=highest)
    grad_tokens = (jnp.einsum("tec,ecd->td", slot_table, input_wide) + router_back).astype(
        jnp.bfloat16
    )
    return (mixed, grad_tokens, grad_router, grad_gate, grad_up, grad_down)


def solution(mesh):
    return jax.shard_map(
        local,
        mesh=mesh,
        in_specs=(
            P(("dp", "expert"), None),
            P(("dp", "expert"), None),
            P(),
            P(None, "expert"),
            P(None, "expert"),
            P(None, "expert"),
            P(("dp", "expert"), None),
        ),
        out_specs=(
            P(("dp", "expert"), None),
            P(("dp", "expert"), None),
            P(),
            P("dp", "expert"),
            P("dp", "expert"),
            P("dp", "expert"),
        ),
        check_vma=False,
    )
```

profile of v0, /device:TPU:1, one launch (start us, length us, event | category | flops | bytes accessed | tf_op | source)
XLA Modules:
  0.0 811.4 jit_solution(12839090901430853241)
XLA Ops:
  10.7 82.5 %all_to_all.21 = bf16[32,7,2560]{2,1,0:T(8,128)(2,1)} all-to-all(bf16[32,7,2560]{2,1,0:T(8,128)(2,1)S(1)} %bitcast.58), channel_id=1, replica_groups=mesh['dp'=16,'expert'=32] {'expert'}, dimensions={0} | all-to-all | bytes 2293760 | tf_op jit(solution)/shard_map/all_to_all | solution.py:73
  93.2 1.5 reshape.115
  94.7 1.9 fusion.22
  96.6 1.2 multiply_convert_fusion.3
  97.8 1.6 convolution_convert_fusion.3
  99.4 2.3 reshape.116
  101.7 8.7 %all-to-all-start.1 = ((bf16[32,7,2560]{2,1,0:T(8,128)(2,1)}), bf16[32,7,2560]{2,1,0:T(8,128)(2,1)}, u32[]{:S(2)}, u32[]{:S(2)}) async-start(bf16[32,7,2560]{2,1,0:T(8,128)(2,1)} %reshape.116), calls=%async_computation.1 | async-start | bytes 2621440 | tf_op jit(solution)/shard_map/all_to_all | solution.py:81
  112.0 36.9 %all-to-all-done.1 = bf16[32,7,2560]{2,1,0:T(8,128)(2,1)} async-done(((bf16[32,7,2560]{2,1,0:T(8,128)(2,1)}), bf16[32,7,2560]{2,1,0:T(8,128)(2,1)}, u32[]{:S(2)}, u32[]{:S(2)}) %all-to-all-start.1) | async-done | bytes 1146912 | tf_op jit(solution)/shard_map/all_to_all | solution.py:81
  148.9 1.6 bitcast_reduce_fusion.1
  150.5 1.1 multiply_reduce_fusion
  152.9 1.4 copy.51
  156.3 74.3 %all_to_all.22 = bf16[32,7,2560]{2,1,0:T(8,128)(2,1)} all-to-all(bf16[32,7,2560]{2,1,0:T(8,128)(2,1)S(1)} %bitcast.59), channel_id=1, replica_groups=mesh['dp'=16,'expert'=32] {'expert'}, dimensions={0} | all-to-all | bytes 2293760 | tf_op jit(solution)/shard_map/all_to_all | solution.py:107
  230.5 2.3 reshape.120
  232.9 1.9 convolution_convert_fusion
  236.4 2.1 pad_maximum_fusion
  238.5 6.3 copy.60
  244.8 1.3 copy-done.1
  248.0 1.3 reshape.121
  249.3 28.4 %all-to-all-start.3 = ((bf16[32,7,2560]{2,1,0:T(8,128)(2,1)}), bf16[32,7,2560]{2,1,0:T(8,128)(2,1)S(1)}, u32[]{:S(2)}, u32[]{:S(2)}) async-start(bf16[32,7,2560]{2,1,0:T(8,128)(2,1)} %reshape.121), calls=%async_computation.3 | async-start | bytes 2621440 | tf_op jit(solution)/shard_map/all_to_all | solution.py:32
  279.8 56.8 %all-to-all-done.3 = bf16[32,7,2560]{2,1,0:T(8,128)(2,1)S(1)} async-done(((bf16[32,7,2560]{2,1,0:T(8,128)(2,1)}), bf16[32,7,2560]{2,1,0:T(8,128)(2,1)S(1)}, u32[]{:S(2)}, u32[]{:S(2)}) %all-to-all-start.3) | async-done | bytes 1146912 | tf_op jit(solution)/shard_map/all_to_all | solution.py:32
  337.9 75.4 %reduce-scatter.4.cloned.1.call-done = bf16[160,768]{1,0:T(8,128)(2,1)} async-done(((bf16[2560,768]{1,0:T(8,128)(2,1)}), bf16[160,768]{1,0:T(8,128)(2,1)}) %reduce-scatter.4.cloned.1.call-update) | async-done | bytes 245776
  413.3 1.1 copy.61
  416.8 385.5 %all-reduce.2.cloned.1.call-done = f32[2560,8]{0,1:T(8,128)} async-done(((f32[2560,8]{0,1:T(8,128)}), f32[2560,8]{0,1:T(8,128)}) %all-reduce.2.cloned.1.call-update) | async-done | bytes 81936 | tf_op jit(solution)/shard_map/psum | solution.py:102
  802.4 1.5 copy.78
  (74 shorter events, 16.8 us)
Async XLA Ops:
  8.0 89.8 %copy-start = (bf16[2560,256]{1,0:T(8,128)(2,1)S(1)}, bf16[2560,256]{1,0:T(8,128)(2,1)}, u32[]{:S(2)}) copy-start(bf16[2560,256]{1,0:T(8,128)(2,1)} %param.12) | copy-start | bytes 3932164
  94.7 1.9 copy-start.3
  96.6 1.2 copy-start.8
  101.7 8.8 %copy-start.5 = (bf16[8,2560]{1,0:T(8,128)(2,1)S(1)}, bf16[8,2560]{1,0:T(8,128)(2,1)}, u32[]{:S(2)}) copy-start(bf16[8,2560]{1,0:T(8,128)(2,1)} %param.7) | copy-start | bytes 122884
  101.7 8.8 %copy-start.6 = (f32[2560,8]{0,1:T(8,128)S(1)}, f32[2560,8]{0,1:T(8,128)}, u32[]{:S(2)}) copy-start(f32[2560,8]{0,1:T(8,128)} %param.9) | copy-start | bytes 245764
  101.7 47.2 %all-to-all-start.1 = ((bf16[32,7,2560]{2,1,0:T(8,128)(2,1)}), bf16[32,7,2560]{2,1,0:T(8,128)(2,1)}, u32[]{:S(2)}, u32[]{:S(2)}) async-start(bf16[32,7,2560]{2,1,0:T(8,128)(2,1)} %reshape.116), calls=%async_computation.1 | async-start | bytes 2621440 | tf_op jit(solution)/shard_map/all_to_all | solution.py:81
  110.4 303.0 %reduce-scatter.4.cloned.1.call-start = ((), (), s32[]{:S(2)}) async-start(), calls=%async_computation.6 | async-start | bytes 4177920
  148.9 2.8 copy-start.12
  151.8 0.5 copy-start.13
  155.4 0.6 copy-start.10
  232.9 1.9 copy-start.2
  232.9 2.0 copy-start.9
  232.9 2.0 copy-start.15
  244.8 1.3 copy-start.1
  246.1 1.3 copy-start.4
  249.3 28.5 %copy-start.14 = (f32[8]{0:T(128)S(1)}, f32[8]{0:T(128)}, u32[]{:S(2)}) copy-start(f32[8]{0:T(128)} %copy-done.13) | copy-start | bytes 100
  249.3 29.5 %copy-start.11 = (f32[8,1,8,7]{2,1,3,0:T(1,128)S(1)}, f32[8,1,8,7]{2,1,3,0:T(1,128)}, u32[]{:S(2)}) copy-start(f32[8,1,8,7]{2,1,3,0:T(1,128)} %copy-done.10) | copy-start | bytes 5380
  249.3 87.2 %all-to-all-start.3 = ((bf16[32,7,2560]{2,1,0:T(8,128)(2,1)}), bf16[32,7,2560]{2,1,0:T(8,128)(2,1)S(1)}, u32[]{:S(2)}, u32[]{:S(2)}) async-start(bf16[32,7,2560]{2,1,0:T(8,128)(2,1)} %reshape.121), calls=%async_computation.3 | async-start | bytes 2621440 | tf_op jit(solution)/shard_map/all_to_all | solution.py:32
  277.7 524.7 %all-reduce.2.cloned.1.call-start = ((), (), s32[]{:S(2)}) async-start(), calls=%async_computation.5 | async-start | bytes 163840 | tf_op jit(solution)/shard_map/psum | solution.py:102
  277.9 59.2 %copy-start.7 = (f32[2560,8]{0,1:T(8,128)S(1)}, f32[2560,8]{0,1:T(8,128)}, u32[]{:S(2)}) copy-start(f32[2560,8]{0,1:T(8,128)} %param.9) | copy-start | bytes 245764
Sparse Core Ops, SparseCore 0:
  244.9 168.3 reduce-scatter.3
Sparse Core Ops, SparseCore 1:
  284.2 518.1 all-reduce.1
where the time goes:
time: 812 us; the launch traced here: 811 us
  waiting for transfers between devices  555 us (68%)
  blocking collectives  157 us (19%)
  starting transfers between devices  37.2 us (5%)
  local copies, waits for them, and re-layouts  24.5 us (3%)
  matrix products  16.2 us (2%)
  between operations  15.8 us (2%)
    psum x1, waiting for transfers between devices, local(): grad_router = lax.psum(router_part, ('dp', 'expert'))  386 us
    all_to_all x1, blocking collectives, local(): lax.all_to_all(outgoing_all, 'expert', split_axis=0, concat_axis=0, tiled...  82.5 us
    unnamed x3, waiting for transfers between devices  75.4 us
    all_to_all x1, blocking collectives, local(): lax.all_to_all(grad_outgoing_all, 'expert', split_axis=0, concat_axis=0,...  74.3 us
    all_to_all x1, waiting for transfers between devices, return_grads(): lax.all_to_all(input_part, 'expert', split_axis=0, concat_axis=0, tiled=T...  56.8 us
    all_to_all x1, waiting for transfers between devices, local(): lax.all_to_all(output, 'expert', split_axis=0, concat_axis=0, tiled=True)  36.9 us
    all_to_all x1, starting transfers between devices, return_grads(): lax.all_to_all(input_part, 'expert', split_axis=0, concat_axis=0, tiled=T...  28.4 us
  transfers between devices with their start and end apart: 4, of which 4 were waited for; matrix products, arithmetic and copies ran while one was open for 1% of the time, Pallas kernels for 0%

commit v1 on v0

v1 whole, which is shorter than its diff:
```python
import functools

import jax
import jax.numpy as jnp
from jax import lax
from jax.experimental import pallas as pl
from jax.experimental.pallas import tpu as pltpu
from jax.sharding import PartitionSpec as P

NY = 4
NZ = 4
MESH = pl.DeviceIdType.MESH
VMEM = pl.BlockSpec(memory_space=pltpu.VMEM)
F32 = jnp.float32
BF16 = jnp.bfloat16


def greet(axis, peers):
    barrier = pltpu.get_barrier_semaphore()
    for peer in peers:
        pl.semaphore_signal(barrier, inc=1, device_id={axis: peer}, device_id_type=MESH)
    pl.semaphore_wait(barrier, len(peers))


def group_place():
    j = lax.axis_index("expert")
    core = lax.rem(j, 2)
    zh = lax.rem(lax.div(j, 2), NZ)
    y = lax.div(j, 2 * NZ)
    return j, y, zh, core


def member(y, zh, core):
    return (lax.rem(y, NY) * NZ + lax.rem(zh, NZ)) * 2 + core


def gather_kernel(x_ref, c_ref, m_ref, xo, co, mo, send_sem, recv_sem, local_sem):
    j, y, zh, core = group_place()
    z_up, z_down = member(y, zh + 1, core), member(y, zh + 3, core)
    y_up, y_down = member(y + 1, zh, core), member(y + 3, zh, core)
    twin = member(y, zh, 1 - core)
    greet("expert", (z_up, z_down, y_up, y_down, twin))
    ins, outs = (x_ref, c_ref, m_ref), (xo, co, mo)
    used = [0, 0, 0]
    sent = []

    def send(a, block, target, own=False):
        copy = pltpu.make_async_remote_copy(
            src_ref=ins[a] if own else outs[a].at[block],
            dst_ref=outs[a].at[block],
            send_sem=send_sem.at[a, used[a]],
            recv_sem=recv_sem.at[a, block],
            device_id={"expert": target},
            device_id_type=MESH,
        )
        used[a] += 1
        copy.start()
        sent.append(copy)

    def arrive(a, block):
        pltpu.make_async_remote_copy(
            src_ref=outs[a].at[block],
            dst_ref=outs[a].at[block],
            send_sem=send_sem.at[a, 0],
            recv_sem=recv_sem.at[a, block],
            device_id={"expert": twin},
            device_id_type=MESH,
        ).wait_recv()

    def at(dy, dz):
        return member(y + dy, zh + dz, core)

    for a in (0, 2, 1):
        send(a, j, z_up, True)
        send(a, j, z_down, True)
    for a in (0, 2, 1):
        send(a, j, y_up, True)
        send(a, j, y_down, True)
        send(a, j, twin, True)
    held = [pltpu.make_async_copy(ins[a], outs[a].at[j], local_sem.at[a]) for a in range(3)]
    for copy in held:
        copy.start()

    def spread(a, dz):
        block = at(0, dz)
        send(a, block, y_up)
        send(a, block, y_down)
        send(a, block, twin)

    def side(dz):
        for a in (0, 2):
            arrive(a, at(3, dz))
            send(a, at(3, dz), y_up)
            send(a, at(3, dz), twin)
        arrive(1, at(1, dz))
        send(1, at(1, dz), y_down)
        send(1, at(1, dz), twin)
        for a in (0, 2):
            arrive(a, at(1, dz))
            send(a, at(1, dz), twin)
        arrive(1, at(3, dz))
        send(1, at(3, dz), twin)

    def far(dz):
        for a in (0, 2, 1):
            arrive(a, at(2, dz))
            send(a, at(2, dz), twin)

    for a in (0, 2):
        arrive(a, at(0, 3))
        send(a, at(0, 3), z_up)
        spread(a, 3)
    for a in (0, 2):
        arrive(a, at(0, 1))
        spread(a, 1)
    arrive(1, at(0, 1))
    send(1, at(0, 1), z_down)
    spread(1, 1)
    arrive(1, at(0, 3))
    spread(1, 3)
    side(0)
    for a in (0, 2, 1):
        arrive(a, at(0, 2))
        spread(a, 2)
    far(0)
    side(3)
    side(1)
    far(3)
    far(1)
    side(2)
    far(2)
    for i in range(NY * NZ):
        for a in range(3):
            arrive(a, 2 * i + 1 - core)
    for copy in held:
        copy.wait()
    for copy in sent:
        copy.wait_send()


def gather(x, c, m):
    shapes = [jax.ShapeDtypeStruct((2 * NY * NZ, *a.shape), a.dtype) for a in (x, c, m)]
    return pl.pallas_call(
        gather_kernel,
        out_shape=shapes,
        in_specs=[VMEM] * 3,
        out_specs=[VMEM] * 3,
        scratch_shapes=[
            pltpu.SemaphoreType.DMA((3, 31)),
            pltpu.SemaphoreType.DMA((3, 32)),
            pltpu.SemaphoreType.DMA((3,)),
        ],
        compiler_params=pltpu.CompilerParams(collective_id=0, has_side_effects=True),
        name="group_gather",
    )(x, c, m)


def remote(src, dst, send_sem, recv_sem, axis, target):
    return pltpu.make_async_remote_copy(
        src_ref=src, dst_ref=dst, send_sem=send_sem, recv_sem=recv_sem,
        device_id={axis: target}, device_id_type=MESH,
    )


def return_kernel(pm, pn, gp, mo, no, go, cbuf, q, s1, fy, r, s1z, fz, r2,
                  cs, cr, ys, yr, zs, zr, gs, gr, gl):
    j, y, zh, core = group_place()
    z_up, z_down = member(y, zh + 1, core), member(y, zh + 3, core)
    y_up, y_down = member(y + 1, zh, core), member(y + 3, zh, core)
    twin = member(y, zh, 1 - core)
    total = 2 * NY * NZ
    barrier = pltpu.get_barrier_semaphore()

    @pl.loop(1, total)
    def _(i):
        pl.semaphore_signal(barrier, inc=1, device_id={"expert": lax.rem(j + i, total)},
                            device_id_type=MESH)

    pl.semaphore_wait(barrier, total - 1)
    parts = (pm, pn)
    sent = []

    def go_on(copy):
        copy.start()
        sent.append(copy)
        return copy

    core_copy = {}
    for dy in (2, 1, 3, 0):
        yy = lax.rem(y + dy, NY)
        for a in range(2):
            core_copy[a, dy] = go_on(remote(parts[a].at[yy, :, 1 - core], cbuf.at[a, yy],
                                            cs.at[a, dy], cr.at[a, yy], "expert", twin))

    def pull_copy(i):
        peer = lax.rem(j + i, total)
        return remote(gp, go.at[j], gs.at[i], gr.at[j], "expert", peer)

    @pl.loop(1, total)
    def _(i):
        pull_copy(i).start()

    keep = pltpu.make_async_copy(gp, go.at[j], gl)
    keep.start()

    def add_core(a, dy):
        yy = lax.rem(y + dy, NY)
        remote(cbuf.at[a, yy], cbuf.at[a, yy], cs.at[a, dy], cr.at[a, yy], "expert", twin).wait_recv()

        @pl.loop(0, NZ)
        def _(k):
            q[a, yy, k] = (parts[a][yy, k, core].astype(F32) + cbuf[a, yy, k].astype(F32)).astype(BF16)

    y2, y1, y3 = lax.rem(y + 2, NY), lax.rem(y + 1, NY), lax.rem(y + 3, NY)
    for a in range(2):
        add_core(a, 2)
        go_on(remote(q.at[a, y2], s1.at[a], ys.at[a, 0], yr.at[a, 0], "expert", (y_up, y_down)[a]))
    for dy in (1, 3):
        for a in range(2):
            add_core(a, dy)
    go_on(remote(q.at[1, y1], fy.at[1, 0], ys.at[1, 1], yr.at[1, 1], "expert", y_up))
    go_on(remote(q.at[0, y3], fy.at[0, 1], ys.at[0, 2], yr.at[0, 2], "expert", y_down))
    for a in range(2):
        near = (y1, y3)[a]
        remote(s1.at[a], s1.at[a], ys.at[a, 0], yr.at[a, 0], "expert", twin).wait_recv()

        @pl.loop(0, NZ)
        def _(k):
            s1[a, k] = (q[a, near, k].astype(F32) + s1[a, k].astype(F32)).astype(BF16)

        go_on(remote(s1.at[a], fy.at[a, a], ys.at[a, 1 + a], yr.at[a, 1 + a], "expert",
                     (y_up, y_down)[a]))
    for a in range(2):
        add_core(a, 0)
        for side in range(2):
            remote(fy.at[a, side], fy.at[a, side], ys.at[a, 0], yr.at[a, 1 + side], "expert",
                   twin).wait_recv()

        @pl.loop(0, NZ)
        def _(k):
            r[a, k] = (q[a, y, k].astype(F32) + fy[a, 0, k].astype(F32)
                       + fy[a, 1, k].astype(F32)).astype(BF16)

    h2, h1, h3 = lax.rem(zh + 2, NZ), lax.rem(zh + 1, NZ), lax.rem(zh + 3, NZ)
    for a in range(2):
        go_on(remote(r.at[a, h2], s1z.at[a], zs.at[a, 0], zr.at[a, 0], "expert", (z_up, z_down)[a]))
    go_on(remote(r.at[1, h1], fz.at[1, 0], zs.at[1, 1], zr.at[1, 1], "expert", z_up))
    go_on(remote(r.at[0, h3], fz.at[0, 1], zs.at[0, 2], zr.at[0, 2], "expert", z_down))
    for a in range(2):
        near = (h1, h3)[a]
        remote(s1z.at[a], s1z.at[a], zs.at[a, 0], zr.at[a, 0], "expert", twin).wait_recv()
        r2[a] = (r[a, near].astype(F32) + s1z[a].astype(F32)).astype(BF16)
        go_on(remote(r2.at[a], fz.at[a, a], zs.at[a, 1 + a], zr.at[a, 1 + a], "expert",
                     (z_up, z_down)[a]))
    outs = (mo, no)
    for a in range(2):
        for side in range(2):
            remote(fz.at[a, side], fz.at[a, side], zs.at[a, 0], zr.at[a, 1 + side], "expert",
                   twin).wait_recv()
        whole = r[a, zh].astype(F32) + fz[a, 0].astype(F32) + fz[a, 1].astype(F32)
        outs[a][...] = whole.astype(outs[a].dtype)

    @pl.loop(1, total)
    def _(i):
        source = lax.rem(j + i, total)
        remote(gp, go.at[source], gs.at[i], gr.at[source], "expert", twin).wait_recv()
        pull_copy(i).wait_send()

    keep.wait()
    for copy in sent:
        copy.wait_send()


def give_back(pm, pn, gp):
    d = pm.shape[-1]
    total = 2 * NY * NZ
    dma = pltpu.SemaphoreType.DMA
    return pl.pallas_call(
        return_kernel,
        out_shape=[
            jax.ShapeDtypeStruct((8, d), BF16),
            jax.ShapeDtypeStruct((8, d), F32),
            jax.ShapeDtypeStruct((total, *gp.shape), F32),
        ],
        in_specs=[VMEM] * 3,
        out_specs=[VMEM] * 3,
        scratch_shapes=[
            pltpu.VMEM((2, NY, NZ, 8, d), BF16),
            pltpu.VMEM((2, NY, NZ, 8, d), BF16),
            pltpu.VMEM((2, NZ, 8, d), BF16),
            pltpu.VMEM((2, 2, NZ, 8, d), BF16),
            pltpu.VMEM((2, NZ, 8, d), BF16),
            pltpu.VMEM((2, 8, d), BF16),
            pltpu.VMEM((2, 2, 8, d), BF16),
            pltpu.VMEM((2, 8, d), BF16),
            dma((2, NY)), dma((2, NY)), dma((2, 3)), dma((2, 3)), dma((2, 3)), dma((2, 3)),
            dma((total,)), dma((total,)), dma,
        ],
        compiler_params=pltpu.CompilerParams(collective_id=1, has_side_effects=True),
        name="group_return",
    )(pm, pn, gp)


def reduce_kernel(w0, w1, w2, g, o0, o1, o2, go, s1, fx, aug, u, zbuf, gx, gsum, gz, gtot,
                  xs, xr, zs, zr, gs, gr, gl):
    dev = lax.axis_index("dp")
    x, zl = lax.div(dev, 4), lax.rem(dev, 4)

    def at(xx, zz):
        return lax.rem(xx, 4) * 4 + lax.rem(zz, 4)

    x_up, x_down = at(x + 1, zl), at(x + 3, zl)
    greet("dp", [at(x + d, zl) for d in (1, 2, 3)] + [at(x, zl + d) for d in (1, 2, 3)])
    ws, outs = (w0, w1, w2), (o0, o1, o2)
    x1, x2, x3 = lax.rem(x + 1, 4), lax.rem(x + 2, 4), lax.rem(x + 3, 4)
    lo, hi = pl.ds(0, 2), pl.ds(2, 2)
    cols = gx.shape[-1]
    sent = []

    def go_on(copy):
        copy.start()
        sent.append(copy)

    def landed(ref, sem):
        remote(ref, ref, sem, sem, "dp", x_up).wait_recv()

    def first(p):
        go_on(remote(ws[p].at[x2, lo], s1.at[p, 0], xs.at[p, 0], xr.at[p, 0], "dp", x_up))
        go_on(remote(ws[p].at[x2, hi], s1.at[p, 1], xs.at[p, 1], xr.at[p, 1], "dp", x_down))

    def plain(p):
        go_on(remote(ws[p].at[x1, hi], fx.at[p, 0, 1], xs.at[p, 2], xr.at[p, 2], "dp", x_up))
        go_on(remote(ws[p].at[x3, lo], fx.at[p, 1, 0], xs.at[p, 3], xr.at[p, 3], "dp", x_down))

    def passed(p):
        for h in range(2):
            landed(s1.at[p, h], xr.at[p, h])
            near = (x1, x3)[h]
            for k in range(2):
                aug[p, h, k] = (ws[p][near, 2 * h + k].astype(F32)
                                + s1[p, h, k].astype(F32)).astype(BF16)
            go_on(remote(aug.at[p, h], fx.at[p, h, h], xs.at[p, 4 + h], xr.at[p, 4 + h], "dp",
                         (x_up, x_down)[h]))

    def lane(xx):
        return pl.ds(pl.multiple_of(lax.rem(xx, 4) * cols, cols), cols)

    def across(p):
        for i in (2, 3, 4, 5):
            ref = (fx.at[p, 0, 1], fx.at[p, 1, 0], fx.at[p, 0, 0], fx.at[p, 1, 1])[i - 2]
            landed(ref, xr.at[p, i])
        for k in range(4):
            u[p, k] = (ws[p][x, k].astype(F32) + fx[p, 0, k // 2, k % 2].astype(F32)
                       + fx[p, 1, k // 2, k % 2].astype(F32)).astype(BF16)
        for d in (2, 1, 3):
            go_on(remote(u.at[p, lax.rem(zl + d, 4)], zbuf.at[p, d - 1], zs.at[p, d - 1],
                         zr.at[p, d - 1], "dp", at(x, zl + d)))

    first(0)
    plain(0)
    for d in (1, 2, 3):
        go_on(remote(g.at[:, lane(x + d)], gx.at[d - 1], gs.at[0, d - 1], gr.at[0, d - 1], "dp",
                     at(x + d, zl)))
    first(1)
    passed(0)
    plain(1)
    first(2)
    for d in range(3):
        landed(gx.at[d], gr.at[0, d])
    gsum[...] = g[:, lane(x)] + gx[0] + gx[1] + gx[2]
    for d in (1, 2, 3):
        go_on(remote(gsum, gz.at[d - 1], gs.at[1, d - 1], gr.at[1, d - 1], "dp", at(x, zl + d)))
    passed(1)
    plain(2)
    across(0)
    for d in range(3):
        landed(gz.at[d], gr.at[1, d])
    gtot[...] = gsum[...] + gz[0] + gz[1] + gz[2]
    for d in (1, 2, 3):
        go_on(remote(gtot, go.at[:, lane(x)], gs.at[2, d - 1], gr.at[2, d - 1], "dp", at(x + d, zl)))
    own = pltpu.make_async_copy(gtot, go.at[:, lane(x)], gl)
    own.start()
    passed(2)
    across(1)
    across(2)
    for p in range(3):
        for d in range(3):
            landed(zbuf.at[p, d], zr.at[p, d])
        outs[p][...] = (u[p, zl].astype(F32) + zbuf[p, 0].astype(F32)
                        + zbuf[p, 1].astype(F32) + zbuf[p, 2].astype(F32))
    for d in range(3):
        landed(go.at[:, lane(x + 3 - d)], gr.at[2, d])
    own.wait()
    for copy in sent:
        copy.wait_send()


def reduce_weights(dws, g):
    rows, f = dws[0].shape
    n = rows // 16
    ws = [w.reshape(4, 4, n, f) for w in dws]
    cols = g.shape[1] // 4
    dma = pltpu.SemaphoreType.DMA
    return pl.pallas_call(
        reduce_kernel,
        out_shape=[jax.ShapeDtypeStruct((n, f), F32)] * 3 + [jax.ShapeDtypeStruct(g.shape, F32)],
        in_specs=[VMEM] * 4,
        out_specs=[VMEM] * 4,
        scratch_shapes=[
            pltpu.VMEM((3, 2, 2, n, f), BF16),
            pltpu.VMEM((3, 2, 2, 2, n, f), BF16),
            pltpu.VMEM((3, 2, 2, n, f), BF16),
            pltpu.VMEM((3, 4, n, f), BF16),
            pltpu.VMEM((3, 3, n, f), BF16),
            pltpu.VMEM((3, 8, cols), F32),
            pltpu.VMEM((8, cols), F32),
            pltpu.VMEM((3, 8, cols), F32),
            pltpu.VMEM((8, cols), F32),
            dma((3, 6)), dma((3, 6)), dma((3, 3)), dma((3, 3)), dma((3, 3)), dma((3, 3)), dma,
        ],
        compiler_params=pltpu.CompilerParams(collective_id=2, has_side_effects=True),
        name="weight_reduce",
    )(*ws, g)


def dot(a, b, contract):
    return lax.dot_general(a, b, (contract, ((), ())), preferred_element_type=F32)


def local(tokens, routes, router, w_gate, w_up, w_down, cotangent):
    d = tokens.shape[1]
    experts = router.shape[1]
    f = w_gate.shape[1]
    highest = lax.Precision.HIGHEST
    j = lax.axis_index("expert")
    lanes = jnp.arange(128, dtype=jnp.int32)
    mark = jnp.sum((routes[:, :, None] == lanes).astype(F32), axis=1)
    xg, cg, mg = gather(tokens, cotangent, mark)
    x = xg.reshape(-1, d)
    c = cg.reshape(-1, d)
    mask = mg.reshape(-1, 128)[:, :experts]
    rows = x.shape[0]
    logits = jnp.dot(x.astype(F32), router, precision=highest)
    affinity = jax.nn.sigmoid(logits)
    denominator = jnp.sum(affinity * mask, axis=1, keepdims=True)
    gates = mask * affinity / denominator
    mine = (jnp.arange(experts) == j // 4).astype(F32)
    gate = jnp.sum(gates * mine, axis=1, keepdims=True)
    gate_pre = dot(x, w_gate, ((1,), (0,)))
    up_pre = dot(x, w_up, ((1,), (0,)))
    pull = dot(c, w_down, ((1,), (0,)))
    sigma = jax.nn.sigmoid(gate_pre)
    silu = gate_pre * sigma
    hidden = silu * up_pre
    scaled = (gate * hidden).astype(BF16)
    gate_pull = jnp.sum(hidden * pull, axis=1)
    hidden_grad = gate * pull
    gate_grad = (hidden_grad * up_pre * sigma * (1.0 + gate_pre * (1.0 - sigma))).astype(BF16)
    up_grad = (hidden_grad * silu).astype(BF16)
    out_part = dot(scaled, w_down, ((1,), (1,))).astype(BF16)
    in_part = (dot(gate_grad, w_gate, ((1,), (1,))) + dot(up_grad, w_up, ((1,), (1,)))).astype(BF16)
    dws = [
        dot(x, gate_grad, ((0,), (0,))).astype(BF16),
        dot(x, up_grad, ((0,), (0,))).astype(BF16),
        dot(c, scaled, ((0,), (0,))).astype(BF16),
    ]
    split = (NY, NZ, 2, 8, d)
    mixed, input_sum, pulls = give_back(
        out_part.reshape(split), in_part.reshape(split), gate_pull.reshape(1, rows)
    )
    full_pull = jnp.sum(pulls.reshape(experts, -1, rows), axis=1).T
    mean_pull = jnp.sum(gates * full_pull, axis=1, keepdims=True)
    logit_grad = mask * (full_pull - mean_pull) / denominator * affinity * (1.0 - affinity)
    router_part = lax.dot_general(
        logit_grad, x.astype(F32), (((0,), (0,)), ((), ())), precision=highest
    )
    own = lax.dynamic_slice(logit_grad, (j * 8, 0), (8, experts))
    router_back = lax.dot_general(own, router, (((1,), (1,)), ((), ())), precision=highest)
    grad_tokens = (input_sum + router_back).astype(BF16)
    grad_gate, grad_up, grad_down, grad_router = reduce_weights(dws, router_part)
    return (mixed, grad_tokens, grad_router.T, grad_gate, grad_up, grad_down)


def solution(mesh):
    return jax.shard_map(
        local,
        mesh=mesh,
        in_specs=(
            P(("dp", "expert"), None),
            P(("dp", "expert"), None),
            P(),
            P(None, "expert"),
            P(None, "expert"),
            P(None, "expert"),
            P(("dp", "expert"), None),
        ),
        out_specs=(
            P(("dp", "expert"), None),
            P(("dp", "expert"), None),
            P(),
            P("dp", "expert"),
            P("dp", "expert"),
            P("dp", "expert"),
        ),
        check_vma=False,
    )
```

time: 812 us -> 164 us (0.20)
  waiting for transfers between devices: 555 us -> 0 us
  blocking collectives: 157 us -> 0 us
  Pallas kernels: 0 us -> 131 us
  starting transfers between devices: 37.2 us -> 0 us
  between operations: 15.8 us -> 0.8 us
  local copies, waits for them, and re-layouts: 24.5 us -> 9.58 us
    psum x1 -> x0, waiting for transfers between devices: 386 us -> none  [local(): grad_router = lax.psum(router_part, ('dp', 'expert'))]
    all_to_all x2 -> x0, blocking collectives: 157 us -> none  [the longest x1 82.5 us: local(): lax.all_to_all(outgoing_all, 'expert', split_axis=0, concat_axis=0, tiled...]
    pallas_call x0 -> x3, Pallas kernels: none -> 131 us  [the longest x1 50 us: reduce_weights(): pl.pallas_call(reduce_kernel, out_shape=[jax.ShapeDtypeStruct((n, f), F32...]
    all_to_all x2 -> x0, waiting for transfers between devices: 93.7 us -> none  [the longest x1 56.8 us: return_grads(): lax.all_to_all(input_part, 'expert', split_axis=0, concat_axis=0, tiled=T...]
    unnamed x3 -> x0, waiting for transfers between devices: 75.4 us -> none
    all_to_all x2 -> x0, starting transfers between devices: 37.1 us -> none  [the longest x1 28.4 us: return_grads(): lax.all_to_all(input_part, 'expert', split_axis=0, concat_axis=0, tiled=T...]
    dot_general x17 -> x12, matrix products: 16.2 us -> 17.5 us  [the longest x9 12.7 us: dot(): lax.dot_general(a, b, (contract, ((), ())), preferred_element_type=F32)]
  transfers between devices with their start and end apart: 4 -> 0, of which waited for: 4 -> 0; matrix products, arithmetic and copies ran while one was open for 1% -> 0% of each run, Pallas kernels for 0% -> 0%
where the time goes in v1:
time: 164 us; the launch traced here: 161 us
  Pallas kernels  131 us (80%)
  matrix products  17.5 us (11%)
  local copies, waits for them, and re-layouts  9.58 us (6%)
  other arithmetic  1.66 us (1%)
    pallas_call x1, Pallas kernels, reduce_weights(): pl.pallas_call(reduce_kernel, out_shape=[jax.ShapeDtypeStruct((n, f), F32...  50 us
    pallas_call x1, Pallas kernels, gather(): pl.pallas_call(gather_kernel, out_shape=shapes, in_specs=[VMEM] * 3, out_...  43.9 us
    pallas_call x1, Pallas kernels, give_back(): pl.pallas_call(return_kernel, out_shape=[jax.ShapeDtypeStruct((8, d), BF1...  37.6 us
    dot_general x9, matrix products, dot(): lax.dot_general(a, b, (contract, ((), ())), preferred_element_type=F32)  12.7 us
    unnamed x25, local copies, waits for them, and re-layouts  9.57 us

profile of v1, /device:TPU:1, one launch (start us, length us, event | category | flops | bytes accessed | tf_op | source)
XLA Modules:
  0.0 160.9 jit_solution(17492230737956143551)
XLA Ops:
  0.7 0.9 copy.14
  1.5 0.7 convert_reduce_fusion.m_ref
  2.2 43.9 %group_gather.1 = (bf16[32,8,2560]{2,1,0:T(8,128)(2,1)}, bf16[32,8,2560]{2,1,0:T(8,128)(2,1)}, f32[32,8,128]{2,1,0:T(8,128)}) custom-call(bf16[8,2560]{1,0:T(8,128)(2,1)} %x_ref.1, bf16[8,2560]{1,0:T(8,128)(2,1)} %c_ref.1, f32[8,128]{1,0:T(8,128)} %convert_reduce_fusion.m_ref), custom_call_target="tpu_custom_call" | custom-call | tf_op jit(solution)/shard_map/group_gather/pallas_call | solution.py:143
  46.1 1.1 copy.17
  47.1 2.5 %fusion.35 = (f32[256]{0:T(256)S(1)}, f32[256,8]{0,1:T(8,128)S(1)}, f32[256,8]{0,1:T(8,128)S(1)}) fusion(f32[256,8]{0,1:T(8,128)S(1)} %copy.17, f32[2560,8]{0,1:T(8,128)} %param.9, bf16[32,8,2560]{2,1,0:T(8,128)(2,1)} %get-tuple-element.17), kind=kOutput, calls=%fused_computation.45 | convolution fusion | flops 62924544 | bytes 1418240 | tf_op jit(solution)/shard_map/dot_general | solution.py:443
  49.7 2.0 %fusion.11 = f32[256,256]{0,1:T(8,128)S(1)} fusion(bf16[2560,256]{1,0:T(8,128)(2,1)} %param.10, bf16[32,8,2560]{2,1,0:T(8,128)(2,1)S(1)} %copy-done.1), kind=kOutput, calls=%fused_computation.17 | convolution fusion | flops 335544320 | bytes 2883584 | tf_op jit(solution)/shard_map/dot_general | solution.py:427
  51.8 0.6 fusion.9
  52.4 0.7 copy-done.4
  53.1 1.3 multiply_reduce_fusion
  55.0 1.7 %fusion = bf16[256,2560]{1,0:T(8,128)(2,1)} fusion(f32[256,2560]{1,0:T(8,128)S(1)} %fusion.36, bf16[256,256]{0,1:T(8,128)(2,1)S(1)} %get-tuple-element.31, bf16[2560,256]{1,0:T(8,128)(2,1)S(1)} %copy-done.3), kind=kOutput, calls=%fused_computation.1 | convolution fusion | flops 336855040 | bytes 5373952 | tf_op jit(solution)/shard_map/dot_general | solution.py:427
  56.7 1.6 %convolution_convert_fusion.3 = bf16[256,2560]{1,0:T(8,128)(2,1)} fusion(bf16[256,256]{0,1:T(8,128)(2,1)S(1)} %get-tuple-element.30, bf16[2560,256]{1,0:T(8,128)(2,1)S(1)} %copy-done), kind=kOutput, calls=%fused_computation.5 | convolution fusion | flops 336199680 | bytes 2752512 | tf_op jit(solution)/shard_map/dot_general | solution.py:427
  58.3 37.6 %group_return.1 = (bf16[8,2560]{1,0:T(8,128)(2,1)}, f32[8,2560]{1,0:T(8,128)}, f32[32,1,256]{2,1,0:T(1,128)}) custom-call(bf16[4,4,2,8,2560]{4,3,2,1,0:T(8,128)(2,1)} %bitcast.70, bf16[4,4,2,8,2560]{4,3,2,1,0:T(8,128)(2,1)} %bitcast.71, f32[1,256]{1,0:T(1,128)} %bitcast.74), custom_call_target="tpu_custom_call" | custom-call | tf_op jit(solution)/shard_map/group_return/pallas_call | solution.py:278
  95.9 0.8 reduce
  96.8 1.3 fusion.5.g
  98.1 1.6 %convolution_convert_fusion.2 = bf16[2560,256]{1,0:T(8,128)(2,1)} fusion(bf16[256,256]{0,1:T(8,128)(2,1)S(1)} %get-tuple-element.29, bf16[32,8,2560]{2,1,0:T(8,128)(2,1)S(1)} %copy-done.1), kind=kOutput, calls=%fused_computation.4 | convolution fusion | flops 336199680 | bytes 2752512 | tf_op jit(solution)/shard_map/dot_general | solution.py:427
  99.7 1.6 %convolution_convert_fusion.1 = bf16[2560,256]{1,0:T(8,128)(2,1)} fusion(bf16[256,256]{0,1:T(8,128)(2,1)S(1)} %get-tuple-element.31, bf16[32,8,2560]{2,1,0:T(8,128)(2,1)S(1)} %copy-done.1), kind=kOutput, calls=%fused_computation.3 | convolution fusion | flops 336199680 | bytes 2752512 | tf_op jit(solution)/shard_map/dot_general | solution.py:427
  101.4 1.6 %convolution_convert_fusion = bf16[2560,256]{1,0:T(8,128)(2,1)} fusion(bf16[256,256]{0,1:T(8,128)(2,1)S(1)} %get-tuple-element.30, bf16[32,8,2560]{2,1,0:T(8,128)(2,1)S(1)} %copy-done.5), kind=kOutput, calls=%fused_computation.2 | convolution fusion | flops 336199680 | bytes 2752512 | tf_op jit(solution)/shard_map/dot_general | solution.py:427
  103.0 50.0 %weight_reduce.1 = (f32[160,256]{1,0:T(8,128)}, f32[160,256]{1,0:T(8,128)}, f32[160,256]{1,0:T(8,128)}, f32[8,2560]{1,0:T(8,128)}) custom-call(bf16[4,4,160,256]{3,2,1,0:T(8,128)(2,1)} %bitcast.67, bf16[4,4,160,256]{3,2,1,0:T(8,128)(2,1)} %bitcast.68, bf16[4,4,160,256]{3,2,1,0:T(8,128)(2,1)} %bitcast.69, f32[8,2560]{1,0:T(8,128)} %fusion.5.g), custom_call_target="tpu_custom_call" | custom-call | tf_op jit(solution)/shard_map/weight_reduce/pallas_call | solution.py:404
  153.0 1.0 fusion.1
  154.0 0.6 copy.23
  154.6 1.5 copy.24
  156.2 1.6 copy.25
  157.7 1.6 copy.26
  159.3 1.6 copy.27
  (24 shorter events, 0.8 us)
Async XLA Ops:
  0.6 51.8 %copy-start = (bf16[2560,256]{1,0:T(8,128)(2,1)S(1)}, bf16[2560,256]{1,0:T(8,128)(2,1)}, u32[]{:S(2)}) copy-start(bf16[2560,256]{1,0:T(8,128)(2,1)} %param.12) | copy-start | bytes 3932164
  46.1 3.6 %copy-start.1 = (bf16[32,8,2560]{2,1,0:T(8,128)(2,1)S(1)}, bf16[32,8,2560]{2,1,0:T(8,128)(2,1)}, u32[]{:S(2)}) copy-start(bf16[32,8,2560]{2,1,0:T(8,128)(2,1)} %get-tuple-element.17) | copy-start | bytes 3932164
  49.7 2.1 %copy-start.3 = (bf16[2560,256]{1,0:T(8,128)(2,1)S(1)}, bf16[2560,256]{1,0:T(8,128)(2,1)}, u32[]{:S(2)}) copy-start(bf16[2560,256]{1,0:T(8,128)(2,1)} %param.11) | copy-start | bytes 3932164
  51.8 1.3 copy-start.4
  53.1 1.3 copy-start.2
  99.7 1.6 %copy-start.5 = (bf16[32,8,2560]{2,1,0:T(8,128)(2,1)S(1)}, bf16[32,8,2560]{2,1,0:T(8,128)(2,1)}, u32[]{:S(2)}) copy-start(bf16[32,8,2560]{2,1,0:T(8,128)(2,1)} %get-tuple-element.18) | copy-start | bytes 3932164
  103.0 50.0 %copy-start.6 = (f32[2560,8]{0,1:T(8,128)S(1)}, f32[2560,8]{0,1:T(8,128)}, u32[]{:S(2)}) copy-start(f32[2560,8]{0,1:T(8,128)} %param.9) | copy-start | bytes 245764
  103.0 50.0 %copy-start.7 = (f32[8,2560]{1,0:T(8,128)S(1)}, f32[8,2560]{1,0:T(8,128)}, u32[]{:S(2)}) copy-start(f32[8,2560]{1,0:T(8,128)} %get-tuple-element.20) | copy-start | bytes 245764
  103.0 51.0 %copy-start.8 = (bf16[8,2560]{1,0:T(8,128)(2,1)S(1)}, bf16[8,2560]{1,0:T(8,128)(2,1)}, u32[]{:S(2)}) copy-start(bf16[8,2560]{1,0:T(8,128)(2,1)} %get-tuple-element.39) | copy-start | bytes 122884

commit v2 on v0

v2 whole, which is shorter than its diff:
```python
import jax
import jax.numpy as jnp
from jax import lax
from jax.experimental import pallas as pl
from jax.experimental.pallas import tpu as pltpu
from jax.sharding import PartitionSpec as P

NY = 4
NZ = 4
NX = 4
NL = 4
GROUP = 2 * NY * NZ
MESH = pl.DeviceIdType.MESH
VMEM = pl.BlockSpec(memory_space=pltpu.VMEM)
ANY = pl.BlockSpec(memory_space=pl.ANY)
F32 = jnp.float32
BF16 = jnp.bfloat16


def member(y, zh, core):
    return (lax.rem(y, NY) * NZ + lax.rem(zh, NZ)) * 2 + core


def dot(a, b, contract):
    return lax.dot_general(a, b, (contract, ((), ())), preferred_element_type=F32)


def thirds(a):
    one = a.astype(BF16).astype(F32)
    two = (a - one).astype(BF16).astype(F32)
    return jnp.concatenate([one, two, a - one - two], axis=0).astype(BF16)


def regroup(a):
    n = a.shape[0] // 3
    return a[:n] + a[n : 2 * n] + a[2 * n :]


def layer_kernel(x_ref, c_ref, m_ref, rt, wg_hbm, wu_hbm, wd_hbm,
                 zo, mo, no, go,
                 xg, cg, mg, pg, prow, wts, gate_pre, up_pre, pull, hs, dg, du, lt,
                 part, cbuf, q, s1, fy, r, s1z, fz, r2,
                 dw, s1x, fx, aug, gx, gsum,
                 wsem, as_, ar, al, ms, mr, ps, pr, ml, cs, cr, ys, yr, zs, zr,
                 xs, xr, us, ur, gs, gr, gl):
    j = lax.axis_index("expert")
    core = lax.rem(j, 2)
    zh = lax.rem(lax.div(j, 2), NZ)
    y = lax.div(j, 2 * NZ)
    dev = lax.axis_index("dp")
    x, zl = lax.div(dev, NL), lax.rem(dev, NL)
    d = x_ref.shape[1]
    rows = GROUP * 8

    def place(xx, zz):
        return lax.rem(xx, NX) * NL + lax.rem(zz, NL)

    def at(dy, dz):
        return member(y + dy, zh + dz, core)

    twin = member(y, zh, 1 - core)
    z_up, z_down, y_up, y_down = at(0, 1), at(0, 3), at(1, 0), at(3, 0)
    x_up, x_down = place(x + 1, zl), place(x + 3, zl)

    loads = [pltpu.make_async_copy(w, wts.at[i], wsem.at[i])
             for i, w in enumerate((wg_hbm, wu_hbm, wd_hbm))]
    for copy in loads:
        copy.start()

    barrier = pltpu.get_barrier_semaphore()
    near = [at(0, 1), at(0, 2), at(0, 3), at(1, 0), at(2, 0), at(3, 0), twin]
    wide = [place(x + k, zl) for k in (1, 2, 3)] + [place(x, zl + k) for k in (1, 2, 3)]
    for peer in near:
        pl.semaphore_signal(barrier, inc=1, device_id={"expert": peer}, device_id_type=MESH)
    for peer in wide:
        pl.semaphore_signal(barrier, inc=1, device_id={"dp": peer}, device_id_type=MESH)
    pl.semaphore_wait(barrier, len(near) + len(wide))

    sent = []

    def remote(src, dst, send_sem, recv_sem, axis, target):
        return pltpu.make_async_remote_copy(
            src_ref=src, dst_ref=dst, send_sem=send_sem, recv_sem=recv_sem,
            device_id={axis: target}, device_id_type=MESH,
        )

    def go_on(*args):
        copy = remote(*args)
        copy.start()
        sent.append(copy)

    def landed(ref, sem):
        remote(ref, ref, sem, sem, "expert", twin).wait_recv()

    ins, outs = (x_ref, c_ref), (xg, cg)
    used = [0, 0]

    def send(a, block, target, own=False):
        go_on(ins[a] if own else outs[a].at[block], outs[a].at[block],
              as_.at[a, used[a]], ar.at[a, block], "expert", target)
        used[a] += 1

    def arrive(a, block):
        landed(outs[a].at[block], ar.at[a, block])

    def spread(a, dz):
        for target in (y_up, y_down, twin):
            send(a, at(0, dz), target)

    def side(dz):
        arrive(0, at(3, dz))
        send(0, at(3, dz), y_up)
        send(0, at(3, dz), twin)
        arrive(1, at(1, dz))
        send(1, at(1, dz), y_down)
        send(1, at(1, dz), twin)
        arrive(0, at(1, dz))
        send(0, at(1, dz), twin)
        arrive(1, at(3, dz))
        send(1, at(3, dz), twin)

    def far(dz):
        for a in range(2):
            arrive(a, at(2, dz))
            send(a, at(2, dz), twin)

    class Small:
        def __init__(self, src, out, ssem, rsem, local):
            self.src, self.out, self.ssem, self.rsem, self.used = src, out, ssem, rsem, 0
            self.keep = pltpu.make_async_copy(src, out.at[j], local)

        def send(self, block, target, own=False):
            go_on(self.src if own else self.out.at[block], self.out.at[block],
                  self.ssem.at[self.used], self.rsem.at[block], "expert", target)
            self.used += 1

        def arrive(self, block):
            landed(self.out.at[block], self.rsem.at[block])

        def first(self):
            for k in (1, 2, 3):
                self.send(j, at(0, k), True)
            for k in (1, 2, 3):
                self.send(j, at(k, 0), True)
            self.send(j, twin, True)
            self.keep.start()

        def second(self):
            for k in (1, 3, 2):
                self.arrive(at(0, k))
                for target in (y_up, at(2, 0), y_down, twin):
                    self.send(at(0, k), target)

        def third(self):
            for dz in (0, 1, 3, 2):
                for dy in (1, 3, 2):
                    self.arrive(at(dy, dz))
                    self.send(at(dy, dz), twin)

        def last(self):
            self.keep.wait()
            for i in range(NY * NZ):
                self.arrive(2 * i + 1 - core)

    marks = Small(m_ref, mg, ms, mr, ml.at[0])
    pulls = Small(prow, pg, ps, pr, ml.at[1])

    for a in range(2):
        send(a, j, z_up, True)
        send(a, j, z_down, True)
    marks.first()
    for a in range(2):
        send(a, j, y_up, True)
        send(a, j, y_down, True)
        send(a, j, twin, True)
    held = [pltpu.make_async_copy(ins[a], outs[a].at[j], al.at[a]) for a in range(2)]
    for copy in held:
        copy.start()
    arrive(0, at(0, 3))
    send(0, at(0, 3), z_up)
    spread(0, 3)
    arrive(0, at(0, 1))
    spread(0, 1)
    arrive(1, at(0, 1))
    send(1, at(0, 1), z_down)
    spread(1, 1)
    arrive(1, at(0, 3))
    spread(1, 3)
    side(0)
    marks.second()
    far(0)
    side(3)
    side(1)
    arrive(0, at(0, 2))
    spread(0, 2)
    arrive(1, at(0, 2))
    spread(1, 2)
    marks.third()
    far(3)
    far(1)
    side(2)
    far(2)
    marks.last()
    for copy in loads + held:
        copy.wait()
    for i in range(NY * NZ):
        arrive(0, 2 * i + 1 - core)

    xv, cv = xg.reshape(rows, d), cg.reshape(rows, d)
    mask = jnp.transpose(mg.reshape(rows, 128)[...])[:8]
    logits = regroup(dot(thirds(rt[...]), xv[...], ((1,), (1,))))
    affinity = jax.nn.sigmoid(logits)
    denominator = jnp.sum(affinity * mask, axis=0, keepdims=True)
    gates = mask * affinity / denominator
    wide_gates = jnp.transpose(jnp.concatenate([gates, jnp.zeros((120, rows), F32)], axis=0))
    mine = lax.broadcasted_iota(jnp.int32, wide_gates.shape, 1) == lax.div(j, 4)
    gate = jnp.sum(jnp.where(mine, wide_gates, 0.0), axis=1, keepdims=True)
    gate_pre[...] = dot(xv[...], wts[0], ((1,), (0,)))
    up_pre[...] = dot(xv[...], wts[1], ((1,), (0,)))
    for i in range(NY * NZ):
        arrive(1, 2 * i + 1 - core)
    pull[...] = dot(cv[...], wts[2], ((1,), (0,)))
    sigma = jax.nn.sigmoid(gate_pre[...])
    silu = gate_pre[...] * sigma
    hidden = silu * up_pre[...]
    hs[...] = (gate * hidden).astype(BF16)
    prow[...] = jnp.sum(jnp.transpose(hidden * pull[...]), axis=0, keepdims=True)
    hidden_grad = gate * pull[...]
    dg[...] = (hidden_grad * up_pre[...] * sigma
               * (1.0 + gate_pre[...] * (1.0 - sigma))).astype(BF16)
    du[...] = (hidden_grad * silu).astype(BF16)

    x1, x2, x3 = lax.rem(x + 1, NX), lax.rem(x + 2, NX), lax.rem(x + 3, NX)
    low, high = pl.ds(0, 2), pl.ds(2, 2)
    chunk = d // NX
    cols = chunk

    def weight_part(p, xx):
        left = xv if p else cv
        span = pl.ds(pl.multiple_of(xx * chunk, chunk), chunk)
        value = dot(left[:, span], (hs, dg, du)[p][...], ((0,), (0,)))
        dw[p, xx] = value.astype(BF16).reshape(dw.shape[2:])

    def first(p):
        weight_part(p, x2)
        go_on(dw.at[p, x2, low], s1x.at[p, 0], xs.at[p, 0], xr.at[p, 0], "dp", x_up)
        go_on(dw.at[p, x2, high], s1x.at[p, 1], xs.at[p, 1], xr.at[p, 1], "dp", x_down)

    def plain(p):
        weight_part(p, x1)
        go_on(dw.at[p, x1, high], fx.at[p, 0, 1], xs.at[p, 2], xr.at[p, 2], "dp", x_up)
        weight_part(p, x3)
        go_on(dw.at[p, x3, low], fx.at[p, 1, 0], xs.at[p, 3], xr.at[p, 3], "dp", x_down)

    def passed(p):
        for h in range(2):
            landed(s1x.at[p, h], xr.at[p, h])
            for k in range(2):
                aug[p, h, k] = (dw[p, (x1, x3)[h], 2 * h + k].astype(F32)
                                + s1x[p, h, k].astype(F32)).astype(BF16)
            go_on(aug.at[p, h], fx.at[p, h, h], xs.at[p, 4 + h], xr.at[p, 4 + h], "dp",
                  (x_up, x_down)[h])

    def across(p):
        for i in (2, 3, 4, 5):
            side_, half = ((0, 1), (1, 0), (0, 0), (1, 1))[i - 2]
            landed(fx.at[p, side_, half], xr.at[p, i])
        for k in range(NL):
            dw[p, x, k] = (dw[p, x, k].astype(F32) + fx[p, 0, k // 2, k % 2].astype(F32)
                           + fx[p, 1, k // 2, k % 2].astype(F32)).astype(BF16)
        for k in (2, 1, 3):
            go_on(dw.at[p, x, lax.rem(zl + k, NL)], zo.at[p, k], us.at[p, k - 1],
                  ur.at[p, k - 1], "dp", place(x, zl + k))
        zo[p, 0] = dw[p, x, zl]

    def start_core(a):
        for dy in (2, 1, 3, 0):
            yy = lax.rem(y + dy, NY)
            go_on(part.at[a, yy, :, 1 - core], cbuf.at[a, yy], cs.at[a, dy], cr.at[a, yy],
                  "expert", twin)

    def add_core(a, dy):
        yy = lax.rem(y + dy, NY)
        landed(cbuf.at[a, yy], cr.at[a, yy])

        @pl.loop(0, NZ)
        def _(k):
            q[a, yy, k] = (part[a, yy, k, core].astype(F32)
                           + cbuf[a, yy, k].astype(F32)).astype(BF16)

    y1, y2, y3 = lax.rem(y + 1, NY), lax.rem(y + 2, NY), lax.rem(y + 3, NY)

    def y_first():
        for a in range(2):
            add_core(a, 2)
            go_on(q.at[a, y2], s1.at[a], ys.at[a, 0], yr.at[a, 0], "expert", (y_up, y_down)[a])
        for dy in (1, 3):
            for a in range(2):
                add_core(a, dy)
        go_on(q.at[1, y1], fy.at[1, 0], ys.at[1, 1], yr.at[1, 1], "expert", y_up)
        go_on(q.at[0, y3], fy.at[0, 1], ys.at[0, 2], yr.at[0, 2], "expert", y_down)

    def y_second():
        for a in range(2):
            landed(s1.at[a], yr.at[a, 0])

            @pl.loop(0, NZ)
            def _(k):
                s1[a, k] = (q[a, (y1, y3)[a], k].astype(F32) + s1[a, k].astype(F32)).astype(BF16)

            go_on(s1.at[a], fy.at[a, a], ys.at[a, 1 + a], yr.at[a, 1 + a], "expert",
                  (y_up, y_down)[a])
        for a in range(2):
            add_core(a, 0)

    h1, h2, h3 = lax.rem(zh + 1, NZ), lax.rem(zh + 2, NZ), lax.rem(zh + 3, NZ)

    def z_first():
        for a in range(2):
            for s in range(2):
                landed(fy.at[a, s], yr.at[a, 1 + s])

            @pl.loop(0, NZ)
            def _(k):
                r[a, k] = (q[a, y, k].astype(F32) + fy[a, 0, k].astype(F32)
                           + fy[a, 1, k].astype(F32)).astype(BF16)

            go_on(r.at[a, h2], s1z.at[a], zs.at[a, 0], zr.at[a, 0], "expert", (z_up, z_down)[a])
        go_on(r.at[1, h1], fz.at[1, 0], zs.at[1, 1], zr.at[1, 1], "expert", z_up)
        go_on(r.at[0, h3], fz.at[0, 1], zs.at[0, 2], zr.at[0, 2], "expert", z_down)

    def z_second():
        for a in range(2):
            landed(s1z.at[a], zr.at[a, 0])
            r2[a] = (r[a, (h1, h3)[a]].astype(F32) + s1z[a].astype(F32)).astype(BF16)
            go_on(r2.at[a], fz.at[a, a], zs.at[a, 1 + a], zr.at[a, 1 + a], "expert",
                  (z_up, z_down)[a])

    def z_third(a):
        for s in range(2):
            landed(fz.at[a, s], zr.at[a, 1 + s])
        return r[a, zh].astype(F32) + fz[a, 0].astype(F32) + fz[a, 1].astype(F32)

    def lane(xx):
        return pl.ds(pl.multiple_of(lax.rem(xx, NX) * cols, cols), cols)

    def router_first():
        pulls.last()
        sums = []
        for e in range(8):
            sums.append(pg[4 * e] + pg[4 * e + 1] + pg[4 * e + 2] + pg[4 * e + 3])
        full = jnp.concatenate(sums, axis=0)
        mean = jnp.sum(gates * full, axis=0, keepdims=True)
        lt[...] = mask * (full - mean) / denominator * affinity * (1.0 - affinity)
        value = regroup(dot(thirds(lt[...]), xv[...], ((1,), (0,))))
        for k in range(NX):
            gx[k] = value[:, k * cols : (k + 1) * cols]
        for k in (1, 2, 3):
            go_on(gx.at[lax.rem(x + k, NX)], gx.at[NX + k - 1], gs.at[0, k - 1],
                  gr.at[0, k - 1], "dp", place(x + k, zl))

    def router_second():
        for k in range(3):
            landed(gx.at[NX + k], gr.at[0, k])
        gsum[...] = gx[x] + gx[NX] + gx[NX + 1] + gx[NX + 2]
        for k in (1, 2, 3):
            go_on(gsum, go.at[zl, :, lane(x)], gs.at[1, k - 1], gr.at[1, k - 1], "dp",
                  place(x, zl + k))
        keep = pltpu.make_async_copy(gsum, go.at[zl, :, lane(x)], gl)
        keep.start()
        keep.wait()

    def router_third():
        for k in (1, 2, 3):
            landed(go.at[lax.rem(zl + NL - k, NL), :, lane(x)], gr.at[1, k - 1])
        for k in (1, 2, 3):
            go_on(go.at[:, :, lane(x)], go.at[:, :, lane(x)], gs.at[2, k - 1], gr.at[2, k - 1],
                  "dp", place(x + k, zl))

    def router_last():
        for k in (1, 2, 3):
            landed(go.at[:, :, lane(x + NX - k)], gr.at[2, k - 1])

    first(0)
    pulls.first()
    plain(0)
    part.reshape(2, rows, d)[0] = dot(hs[...], wts[2], ((1,), (1,))).astype(BF16)
    start_core(0)
    part.reshape(2, rows, d)[1] = (dot(dg[...], wts[0], ((1,), (1,)))
                                   + dot(du[...], wts[1], ((1,), (1,)))).astype(BF16)
    start_core(1)
    first(1)
    y_first()
    passed(0)
    plain(1)
    y_second()
    first(2)
    pulls.second()
    passed(1)
    plain(2)
    weight_part(0, x)
    z_first()
    pulls.third()
    across(0)
    router_first()
    weight_part(1, x)
    weight_part(2, x)
    z_second()
    passed(2)
    router_second()
    across(1)
    mo[...] = z_third(0)
    total = z_third(1)
    ours = lax.broadcasted_iota(jnp.int32, (8, rows), 0) + 8 * j
    pick = lax.broadcasted_iota(jnp.int32, (8, rows), 1) == ours
    for e in range(8):
        weight = jnp.sum(jnp.where(pick, lt[e : e + 1, :], 0.0), axis=1, keepdims=True)
        total = total + weight * rt[e : e + 1, :]
    no[...] = total
    router_third()
    across(2)
    router_last()
    for p in range(3):
        for k in range(3):
            landed(zo.at[p, k + 1], ur.at[p, k])
    for copy in sent:
        copy.wait_send()


def layer(tokens, cotangent, mark, router_t, w_gate, w_up, w_down):
    d = tokens.shape[1]
    f = w_gate.shape[1]
    rows = GROUP * 8
    n = d // (NX * NL)
    cols = d // NX
    dma = pltpu.SemaphoreType.DMA
    return pl.pallas_call(
        layer_kernel,
        out_shape=[
            jax.ShapeDtypeStruct((3, NL, n, f), BF16),
            jax.ShapeDtypeStruct((8, d), F32),
            jax.ShapeDtypeStruct((8, d), F32),
            jax.ShapeDtypeStruct((NL, 8, d), F32),
        ],
        in_specs=[VMEM] * 4 + [ANY] * 3,
        out_specs=[VMEM] * 4,
        scratch_shapes=[
            pltpu.VMEM((GROUP, 8, d), BF16),
            pltpu.VMEM((GROUP, 8, d), BF16),
            pltpu.VMEM((GROUP, 8, 128), F32),
            pltpu.VMEM((GROUP, 1, rows), F32),
            pltpu.VMEM((1, rows), F32),
            pltpu.VMEM((3, d, f), BF16),
            pltpu.VMEM((rows, f), F32),
            pltpu.VMEM((rows, f), F32),
            pltpu.VMEM((rows, f), F32),
            pltpu.VMEM((rows, f), BF16),
            pltpu.VMEM((rows, f), BF16),
            pltpu.VMEM((rows, f), BF16),
            pltpu.VMEM((8, rows), F32),
            pltpu.VMEM((2, NY, NZ, 2, 8, d), BF16),
            pltpu.VMEM((2, NY, NZ, 8, d), BF16),
            pltpu.VMEM((2, NY, NZ, 8, d), BF16),
            pltpu.VMEM((2, NZ, 8, d), BF16),
            pltpu.VMEM((2, 2, NZ, 8, d), BF16),
            pltpu.VMEM((2, NZ, 8, d), BF16),
            pltpu.VMEM((2, 8, d), BF16),
            pltpu.VMEM((2, 2, 8, d), BF16),
            pltpu.VMEM((2, 8, d), BF16),
            pltpu.VMEM((3, NX, NL, n, f), BF16),
            pltpu.VMEM((3, 2, 2, n, f), BF16),
            pltpu.VMEM((3, 2, 2, 2, n, f), BF16),
            pltpu.VMEM((3, 2, 2, n, f), BF16),
            pltpu.VMEM((NX + 3, 8, cols), F32),
            pltpu.VMEM((8, cols), F32),
            dma((3,)), dma((2, 31)), dma((2, GROUP)), dma((2,)),
            dma((31,)), dma((GROUP,)), dma((31,)), dma((GROUP,)), dma((2,)),
            dma((2, NY)), dma((2, NY)), dma((2, 3)), dma((2, 3)), dma((2, 3)), dma((2, 3)),
            dma((3, 6)), dma((3, 6)), dma((3, 3)), dma((3, 3)), dma((3, 3)), dma((3, 3)), dma,
        ],
        compiler_params=pltpu.CompilerParams(collective_id=0, has_side_effects=True),
        name="moe_layer",
    )(tokens, cotangent, mark, router_t, w_gate, w_up, w_down)


def finish_kernel(z, m, t, g, mo, to, go, o0, o1, o2):
    mo[...] = m[...].astype(BF16)
    to[...] = t[...].astype(BF16)
    go[...] = g[0] + g[1] + g[2] + g[3]
    for out, p in ((o2, 0), (o0, 1), (o1, 2)):
        out[...] = (z[p, 0].astype(F32) + z[p, 1].astype(F32)
                    + z[p, 2].astype(F32) + z[p, 3].astype(F32))


def finish(z, m, t, g):
    grad = jax.ShapeDtypeStruct(z.shape[2:], F32)
    token = jax.ShapeDtypeStruct(m.shape, BF16)
    return pl.pallas_call(
        finish_kernel,
        out_shape=[token, token, jax.ShapeDtypeStruct(g.shape[1:], F32), grad, grad, grad],
        in_specs=[VMEM] * 4,
        out_specs=[VMEM] * 6,
        name="finish",
    )(z, m, t, g)


def local(tokens, routes, router, w_gate, w_up, w_down, cotangent):
    lanes = jnp.arange(128, dtype=jnp.int32)
    mark = jnp.sum((routes[:, :, None] == lanes).astype(F32), axis=1)
    parts = layer(tokens, cotangent, mark, router.T, w_gate, w_up, w_down)
    mixed, grad_tokens, grad_router, grad_gate, grad_up, grad_down = finish(*parts)
    return (mixed, grad_tokens, grad_router.T, grad_gate, grad_up, grad_down)


def solution(mesh):
    return jax.shard_map(
        local,
        mesh=mesh,
        in_specs=(
            P(("dp", "expert"), None),
            P(("dp", "expert"), None),
            P(),
            P(None, "expert"),
            P(None, "expert"),
            P(None, "expert"),
            P(("dp", "expert"), None),
        ),
        out_specs=(
            P(("dp", "expert"), None),
            P(("dp", "expert"), None),
            P(),
            P("dp", "expert"),
            P("dp", "expert"),
            P("dp", "expert"),
        ),
        check_vma=False,
    )
```

time: 812 us -> 103 us (0.13)
  waiting for transfers between devices: 555 us -> 0 us
  blocking collectives: 157 us -> 0 us
  Pallas kernels: 0 us -> 100 us
  starting transfers between devices: 37.2 us -> 0 us
  local copies, waits for them, and re-layouts: 24.5 us -> 0.77 us
  matrix products: 16.2 us -> 0 us
  between operations: 15.8 us -> 0.64 us
    psum x1 -> x0, waiting for transfers between devices: 386 us -> none  [local(): grad_router = lax.psum(router_part, ('dp', 'expert'))]
    all_to_all x2 -> x0, blocking collectives: 157 us -> none  [the longest x1 82.5 us: local(): lax.all_to_all(outgoing_all, 'expert', split_axis=0, concat_axis=0, tiled...]
    pallas_call x0 -> x2, Pallas kernels: none -> 100 us  [the longest x1 98.3 us: layer(): pl.pallas_call(layer_kernel, out_shape=[jax.ShapeDtypeStruct((3, NL, n, f...]
    all_to_all x2 -> x0, waiting for transfers between devices: 93.7 us -> none  [the longest x1 56.8 us: return_grads(): lax.all_to_all(input_part, 'expert', split_axis=0, concat_axis=0, tiled=T...]
    unnamed x3 -> x0, waiting for transfers between devices: 75.4 us -> none
    all_to_all x2 -> x0, starting transfers between devices: 37.1 us -> none  [the longest x1 28.4 us: return_grads(): lax.all_to_all(input_part, 'expert', split_axis=0, concat_axis=0, tiled=T...]
    dot_general x17 -> x0, matrix products: 16.2 us -> none  [the longest x1 1.94 us: local(): lax.dot_general(grad_flat, hidden_flat, contract, preferred_element_type=...]
    unnamed x39 -> x1, local copies, waits for them, and re-layouts: 15.3 us -> 0.77 us
  transfers between devices with their start and end apart: 4 -> 0, of which waited for: 4 -> 0; matrix products, arithmetic and copies ran while one was open for 1% -> 0% of each run, Pallas kernels for 0% -> 0%
where the time goes in v2:
time: 103 us
  Pallas kernels  100 us (97%)
    pallas_call x1, Pallas kernels, layer(): pl.pallas_call(layer_kernel, out_shape=[jax.ShapeDtypeStruct((3, NL, n, f...  98.3 us
    pallas_call x1, Pallas kernels, finish(): pl.pallas_call(finish_kernel, out_shape=[token, token, jax.ShapeDtypeStru...  2.21 us

profile of v2, /device:TPU:1, one launch (start us, length us, event | category | flops | bytes accessed | tf_op | source)
XLA Modules:
  0.0 102.5 jit_solution(18403028828842758455)
XLA Ops:
  0.6 0.8 copy.13
  1.4 0.7 convert_reduce_fusion.m_ref
  2.1 98.3 %moe_layer.1 = (bf16[3,4,160,256]{3,2,1,0:T(8,128)(2,1)}, f32[8,2560]{1,0:T(8,128)}, f32[8,2560]{1,0:T(8,128)}, f32[4,8,2560]{2,1,0:T(8,128)}) custom-call(bf16[8,2560]{1,0:T(8,128)(2,1)} %x_ref.1, bf16[8,2560]{1,0:T(8,128)(2,1)} %c_ref.1, f32[8,128]{1,0:T(8,128)} %convert_reduce_fusion.m_ref, f32[8,2560]{1,0:T(8,128)} %bitcast.2, bf16[2560,256]{1,0:T(8,128)(2,1)} %wg_hbm.1, ...), custom_call_target="tpu_custom_call" | custom-call | tf_op jit(solution)/shard_map/moe_layer/pallas_call | solution.py:437
  100.3 2.2 %finish.1 = (bf16[8,2560]{1,0:T(8,128)(2,1)}, bf16[8,2560]{1,0:T(8,128)(2,1)}, f32[8,2560]{1,0:T(8,128)}, f32[160,256]{1,0:T(8,128)}, f32[160,256]{1,0:T(8,128)}, /*index=5*/f32[160,256]{1,0:T(8,128)}) custom-call(bf16[3,4,160,256]{3,2,1,0:T(8,128)(2,1)} %get-tuple-element.16.z, f32[8,2560]{1,0:T(8,128)} %get-tuple-element.17.m, ...), custom_call_target="tpu_custom_call" | custom-call | tf_op jit(solution)/shard_map/finish/pallas_call | solution.py:498

commit v3 on v2

v3 whole, which is shorter than its diff:
```python
import jax
import jax.numpy as jnp
from jax import lax
from jax.experimental import pallas as pl
from jax.experimental.pallas import tpu as pltpu
from jax.sharding import PartitionSpec as P

NY = 4
NZ = 4
NX = 4
NL = 4
GROUP = 2 * NY * NZ
MESH = pl.DeviceIdType.MESH
VMEM = pl.BlockSpec(memory_space=pltpu.VMEM)
ANY = pl.BlockSpec(memory_space=pl.ANY)
F32 = jnp.float32
BF16 = jnp.bfloat16


def member(y, zh, core):
    return (lax.rem(y, NY) * NZ + lax.rem(zh, NZ)) * 2 + core


def dot(a, b, contract):
    return lax.dot_general(a, b, (contract, ((), ())), preferred_element_type=F32)


def thirds(a):
    one = a.astype(BF16).astype(F32)
    two = (a - one).astype(BF16).astype(F32)
    return jnp.concatenate([one, two, a - one - two], axis=0).astype(BF16)


def regroup(a):
    n = a.shape[0] // 3
    return a[:n] + a[n : 2 * n] + a[2 * n :]


def layer_kernel(x_hbm, c_hbm, routes_hbm, rt_hbm, wg_hbm, wu_hbm, wd_hbm,
                 wo_hbm, to_hbm, go_hbm,
                 x_ref, c_ref, routes_ref, rt, zo, go, wo, to, gout,
                 xg, cg, mg, m_ref, pg, prow, wts, gate_pre, up_pre, pull, acts, lt,
                 part, cbuf, q, s1, fy, r, s1z, fz, r2,
                 dw, slices, aid, gx, gsum,
                 isem, osem, wsem, as_, ar, al, ms, mr, ps, pr, ml, cs, cr, ys, yr, zs, zr,
                 es, er, ts, tr, xs, xr, vs, vr, us, ur, hs_, hr, gs, gr, gl):
    j = lax.axis_index("expert")
    core = lax.rem(j, 2)
    zh = lax.rem(lax.div(j, 2), NZ)
    y = lax.div(j, 2 * NZ)
    dev = lax.axis_index("dp")
    x, zl = lax.div(dev, NL), lax.rem(dev, NL)
    d = x_ref.shape[1]
    rows = GROUP * 8

    def place(xx, zz):
        return lax.rem(xx, NX) * NL + lax.rem(zz, NL)

    def at(dy, dz):
        return member(y + dy, zh + dz, core)

    twin = member(y, zh, 1 - core)
    z_up, z_down, y_up, y_down = at(0, 1), at(0, 3), at(1, 0), at(3, 0)
    x_up, x_down = place(x + 1, zl), place(x + 3, zl)

    reads = [pltpu.make_async_copy(src, dst, isem.at[i])
             for i, (src, dst) in enumerate(((x_hbm, x_ref), (c_hbm, c_ref),
                                             (routes_hbm, routes_ref), (rt_hbm, rt)))]
    for copy in reads:
        copy.start()
    loads = [pltpu.make_async_copy(w, wts.at[i], wsem.at[i])
             for i, w in enumerate((wg_hbm, wu_hbm, wd_hbm))]
    for copy in loads:
        copy.start()

    barrier = pltpu.get_barrier_semaphore()
    near = [at(0, 1), at(0, 2), at(0, 3), at(1, 0), at(2, 0), at(3, 0), twin]
    wide = [place(x + k, zl) for k in (1, 2, 3)] + [place(x, zl + k) for k in (1, 2, 3)]
    for peer in near:
        pl.semaphore_signal(barrier, inc=1, device_id={"expert": peer}, device_id_type=MESH)
    for peer in wide:
        pl.semaphore_signal(barrier, inc=1, device_id={"dp": peer}, device_id_type=MESH)
    for copy in reads:
        copy.wait()
    lanes = lax.broadcasted_iota(jnp.int32, m_ref.shape, 1)
    m_ref[...] = sum((routes_ref[:, k : k + 1] == lanes).astype(F32)
                     for k in range(routes_ref.shape[1]))
    pl.semaphore_wait(barrier, len(near) + len(wide))

    sent = []

    def remote(src, dst, send_sem, recv_sem, axis, target):
        return pltpu.make_async_remote_copy(
            src_ref=src, dst_ref=dst, send_sem=send_sem, recv_sem=recv_sem,
            device_id={axis: target}, device_id_type=MESH,
        )

    def go_on(*args):
        copy = remote(*args)
        copy.start()
        sent.append(copy)

    def landed(ref, sem):
        remote(ref, ref, sem, sem, "expert", twin).wait_recv()

    ins, outs = (x_ref, c_ref), (xg, cg)
    used = [0, 0]

    def send(a, dy, dz, target, own=False):
        block = lax.rem(y + dy, NY), lax.rem(zh + dz, NZ), core
        go_on(ins[a] if own else outs[a].at[block], outs[a].at[block],
              as_.at[a, used[a]], ar.at[a, member(*block)], "expert", target)
        used[a] += 1

    def arrive(a, dy, dz):
        block = lax.rem(y + dy, NY), lax.rem(zh + dz, NZ), core
        landed(outs[a].at[block], ar.at[a, member(*block)])

    def arrive_twin(a):
        for i in range(NY * NZ):
            landed(outs[a].at[i // NZ, i % NZ, 1 - core], ar.at[a, 2 * i + 1 - core])

    def spread(a, dz, own=False):
        for target in (y_up, y_down, at(2, 0), twin):
            send(a, 0, dz, target, own)

    def from_z(a, dz):
        arrive(a, 0, dz)
        spread(a, dz)

    def from_y(a, dy, dz):
        arrive(a, dy, dz)
        send(a, dy, dz, twin)

    cols = d // NX

    def lane(xx):
        return pl.ds(pl.multiple_of(lax.rem(xx, NX) * cols, cols), cols)

    def slice_out(dz):
        zz = lax.rem(zh + dz, NZ)
        for a in range(2):
            for k in (2, 1, 3):
                go_on(outs[a].at[:, zz, core, :, lane(x + k)], slices.at[a, k - 1, :, zz, core],
                      es.at[a, k - 1, dz], er.at[a, k - 1, zz], "dp", place(x + k, zl))

    def slice_twin(dz):
        zz = lax.rem(zh + dz, NZ)
        for a in range(2):
            for k in (1, 3, 2):
                ref = slices.at[a, k - 1, :, zz, core]
                landed(ref, er.at[a, k - 1, zz])
                go_on(ref, ref, ts.at[a, k - 1, dz], tr.at[a, k - 1, zz], "expert", twin)

    def slice_in(a):
        for k in (1, 3, 2):
            for zz in range(NZ):
                landed(slices.at[a, k - 1, :, zz, 1 - core], tr.at[a, k - 1, zz])

    class Small:
        def __init__(self, src, out, ssem, rsem, local):
            self.src, self.out, self.ssem, self.rsem, self.used = src, out, ssem, rsem, 0
            self.keep = pltpu.make_async_copy(src, out.at[j], local)

        def send(self, block, target, own=False):
            go_on(self.src if own else self.out.at[block], self.out.at[block],
                  self.ssem.at[self.used], self.rsem.at[block], "expert", target)
            self.used += 1

        def arrive(self, block):
            landed(self.out.at[block], self.rsem.at[block])

        def first(self):
            for k in (1, 2, 3):
                self.send(j, at(0, k), True)
            for k in (1, 2, 3):
                self.send(j, at(k, 0), True)
            self.send(j, twin, True)
            self.keep.start()

        def second(self):
            for k in (1, 3, 2):
                self.arrive(at(0, k))
                for target in (y_up, at(2, 0), y_down, twin):
                    self.send(at(0, k), target)

        def third(self):
            for dz in (0, 1, 3, 2):
                for dy in (1, 3, 2):
                    self.arrive(at(dy, dz))
                    self.send(at(dy, dz), twin)

        def last(self):
            self.keep.wait()
            for i in range(NY * NZ):
                self.arrive(2 * i + 1 - core)

    marks = Small(m_ref, mg, ms, mr, ml.at[0])
    pulls = Small(prow, pg, ps, pr, ml.at[1])

    for a in range(2):
        for k in (1, 3, 2):
            send(a, 0, 0, at(0, k), True)
        if a == 0:
            marks.first()
    for a in range(2):
        spread(a, 0, True)
    held = [pltpu.make_async_copy(ins[a], outs[a].at[y, zh, core], al.at[a]) for a in range(2)]
    for copy in held:
        copy.start()
    for a in range(2):
        for dy in (3, 1, 2):
            from_y(a, dy, 0)
    for copy in loads + held:
        copy.wait()
    slice_out(0)
    for a in range(2):
        for dz in (3, 1):
            from_z(a, dz)
    marks.second()
    for dz in (3, 1):
        for a in range(2):
            for dy in (3, 1):
                from_y(a, dy, dz)
    for a in range(2):
        from_z(a, 2)
    for dz in (3, 1):
        for a in range(2):
            from_y(a, 2, dz)
        slice_out(dz)
    marks.third()
    for a in range(2):
        for dy in (3, 1, 2):
            from_y(a, dy, 2)
    slice_out(2)
    marks.last()
    arrive_twin(0)

    xv, cv = xg.reshape(rows, d), cg.reshape(rows, d)
    mask = jnp.transpose(mg.reshape(rows, 128)[...])[:8]
    logits = regroup(dot(thirds(rt[...]), xv[...], ((1,), (1,))))
    affinity = jax.nn.sigmoid(logits)
    denominator = jnp.sum(affinity * mask, axis=0, keepdims=True)
    gates = mask * affinity / denominator
    wide_gates = jnp.transpose(jnp.concatenate([gates, jnp.zeros((120, rows), F32)], axis=0))
    mine = lax.broadcasted_iota(jnp.int32, wide_gates.shape, 1) == lax.div(j, 4)
    gate = jnp.sum(jnp.where(mine, wide_gates, 0.0), axis=1, keepdims=True)
    gate_pre[...] = dot(xv[...], wts[0], ((1,), (0,)))
    up_pre[...] = dot(xv[...], wts[1], ((1,), (0,)))
    arrive_twin(1)
    pull[...] = dot(cv[...], wts[2], ((1,), (0,)))
    sigma = jax.nn.sigmoid(gate_pre[...])
    silu = gate_pre[...] * sigma
    hidden = silu * up_pre[...]
    hs, dg, du = acts.at[0, 0], acts.at[0, 1], acts.at[0, 2]
    hs[...] = (gate * hidden).astype(BF16)
    prow[...] = jnp.sum(jnp.transpose(hidden * pull[...]), axis=0, keepdims=True)
    hidden_grad = gate * pull[...]
    dg[...] = (hidden_grad * up_pre[...] * sigma
               * (1.0 + gate_pre[...] * (1.0 - sigma))).astype(BF16)
    du[...] = (hidden_grad * silu).astype(BF16)

    half = rows // 2
    ends = pl.ds(0, half), pl.ds(half, half)

    def acts_first(p):
        go_on(acts.at[0, p], acts.at[1, p], xs.at[p, 0], xr.at[p, 0], "dp", x_up)
        go_on(acts.at[0, p], acts.at[3, p], xs.at[p, 1], xr.at[p, 1], "dp", x_down)

    def acts_second(p):
        for h in range(2):
            landed(acts.at[(1, 3)[h], p], xr.at[p, h])
            go_on(acts.at[(1, 3)[h], p, ends[h]], acts.at[2, p, ends[h]], vs.at[p, h],
                  vr.at[p, h], "dp", (x_up, x_down)[h])

    def weight_rows(p):
        for h in range(2):
            landed(acts.at[2, p, ends[h]], vr.at[p, h])
        a = 0 if p else 1
        value = dot((cv, xv)[p > 0][:, lane(x)], acts[0, p], ((0,), (0,)))
        for k in (1, 2, 3):
            other = slices.at[a, k - 1].reshape(rows, cols)
            value = value + dot(other[...], acts[k, p], ((0,), (0,)))
        dw[p] = value.astype(BF16).reshape(dw.shape[1:])

    writes = []

    def write(src, dst, i):
        copy = pltpu.make_async_copy(src, dst, osem.at[i])
        copy.start()
        writes.append(copy)

    is_end = jnp.logical_or(zl == 0, zl == NL - 1)

    def hop(p, k, to_aid):
        shard = dw.at[p, lax.rem(zl + k, NL)]
        if to_aid:
            return remote(shard, aid.at[p], hs_.at[p], hr.at[p], "dp", place(x, zl + NL - k))
        return remote(shard, zo.at[p, k], us.at[p, k - 1], ur.at[p, k - 1], "dp",
                      place(x, zl + k))

    def across_first(p):
        for k, end in ((3, 0), (1, NL - 1)):
            @pl.when(zl == end)
            def _():
                hop(p, k, True).start()

            @pl.when(zl != end)
            def _():
                hop(p, k, False).start()

        @pl.when(is_end)
        def _():
            hop(p, 2, False).start()

        zo[p, 0] = dw[p, zl]

        @pl.when(zl == 0)
        def _():
            zo[p, 1] = jnp.zeros(zo.shape[2:], BF16)

        @pl.when(zl == NL - 1)
        def _():
            zo[p, 3] = jnp.zeros(zo.shape[2:], BF16)

    def across_second(p):
        @pl.when(jnp.logical_not(is_end))
        def _():
            landed(aid.at[p], hr.at[p])
            aid[p] = (dw[p, lax.rem(zl + 2, NL)].astype(F32) + aid[p].astype(F32)).astype(BF16)
            remote(aid.at[p], zo.at[p, 2], us.at[p, 1], ur.at[p, 1], "dp",
                   place(x, zl + 2)).start()

    def across_last(p):
        landed(zo.at[p, 2], ur.at[p, 1])
        hop(p, 2, False).wait_send()
        for k, end, none in ((3, 0, NL - 1), (1, NL - 1, 0)):
            @pl.when(zl == end)
            def _():
                hop(p, k, True).wait_send()

            @pl.when(zl != end)
            def _():
                hop(p, k, False).wait_send()

            @pl.when(zl != none)
            def _():
                landed(zo.at[p, k], ur.at[p, k - 1])

        wo[p] = (zo[p, 0].astype(F32) + zo[p, 1].astype(F32)
                 + zo[p, 2].astype(F32) + zo[p, 3].astype(F32))
        write(wo.at[p], wo_hbm.at[p], p)

    def start_core(a):
        for dy in (2, 1, 3, 0):
            yy = lax.rem(y + dy, NY)
            go_on(part.at[a, yy, :, 1 - core], cbuf.at[a, yy], cs.at[a, dy], cr.at[a, yy],
                  "expert", twin)

    def add_core(a, dy):
        yy = lax.rem(y + dy, NY)
        landed(cbuf.at[a, yy], cr.at[a, yy])

        @pl.loop(0, NZ)
        def _(k):
            q[a, yy, k] = (part[a, yy, k, core].astype(F32)
                           + cbuf[a, yy, k].astype(F32)).astype(BF16)

    y1, y2, y3 = lax.rem(y + 1, NY), lax.rem(y + 2, NY), lax.rem(y + 3, NY)

    def row(k):
        return lax.rem(zh + k, NZ)

    def y_start(k):
        zz = row(k)
        for a in range(2):
            go_on(q.at[a, y2, zz], s1.at[a, zz], ys.at[a, 0, k], yr.at[a, 0, k], "expert",
                  (y_up, y_down)[a])

    def y_plain(k):
        zz = row(k)
        go_on(q.at[1, y1, zz], fy.at[1, 0, zz], ys.at[1, 1, k], yr.at[1, 1, k], "expert", y_up)
        go_on(q.at[0, y3, zz], fy.at[0, 1, zz], ys.at[0, 2, k], yr.at[0, 2, k], "expert", y_down)

    def y_first():
        for dy in (2, 1, 3):
            for a in range(2):
                add_core(a, dy)
        y_start(2)
        y_plain(2)
        y_start(1)
        for a in range(2):
            add_core(a, 0)

    def y_pass(k):
        zz = row(k)
        for a in range(2):
            landed(s1.at[a, zz], yr.at[a, 0, k])
            s1[a, zz] = (q[a, (y1, y3)[a], zz].astype(F32) + s1[a, zz].astype(F32)).astype(BF16)
            go_on(s1.at[a, zz], fy.at[a, a, zz], ys.at[a, 1 + a, k], yr.at[a, 1 + a, k], "expert",
                  (y_up, y_down)[a])

    h1, h2, h3 = lax.rem(zh + 1, NZ), lax.rem(zh + 2, NZ), lax.rem(zh + 3, NZ)

    def y_end(k):
        zz = row(k)
        for a in range(2):
            for s in range(2):
                landed(fy.at[a, s, zz], yr.at[a, 1 + s, k])
            r[a, zz] = (q[a, y, zz].astype(F32) + fy[a, 0, zz].astype(F32)
                        + fy[a, 1, zz].astype(F32)).astype(BF16)
            if k == 2:
                go_on(r.at[a, zz], s1z.at[a], zs.at[a, 0], zr.at[a, 0], "expert",
                      (z_up, z_down)[a])
        if k == 1:
            go_on(r.at[1, zz], fz.at[1, 0], zs.at[1, 1], zr.at[1, 1], "expert", z_up)
        if k == 3:
            go_on(r.at[0, zz], fz.at[0, 1], zs.at[0, 2], zr.at[0, 2], "expert", z_down)

    def z_second():
        for a in range(2):
            landed(s1z.at[a], zr.at[a, 0])
            r2[a] = (r[a, (h1, h3)[a]].astype(F32) + s1z[a].astype(F32)).astype(BF16)
            go_on(r2.at[a], fz.at[a, a], zs.at[a, 1 + a], zr.at[a, 1 + a], "expert",
                  (z_up, z_down)[a])

    def z_third(a):
        for s in range(2):
            landed(fz.at[a, s], zr.at[a, 1 + s])
        return r[a, zh].astype(F32) + fz[a, 0].astype(F32) + fz[a, 1].astype(F32)

    def router_first():
        sums = []
        for e in range(8):
            sums.append(pg[4 * e] + pg[4 * e + 1] + pg[4 * e + 2] + pg[4 * e + 3])
        full = jnp.concatenate(sums, axis=0)
        mean = jnp.sum(gates * full, axis=0, keepdims=True)
        lt[...] = mask * (full - mean) / denominator * affinity * (1.0 - affinity)
        value = regroup(dot(thirds(lt[...]), xv[...], ((1,), (0,))))
        for k in range(NX):
            gx[k] = value[:, k * cols : (k + 1) * cols]
        for k in (1, 2, 3):
            go_on(gx.at[lax.rem(x + k, NX)], gx.at[NX + k - 1], gs.at[0, k - 1],
                  gr.at[0, k - 1], "dp", place(x + k, zl))

    def router_second():
        for k in range(3):
            landed(gx.at[NX + k], gr.at[0, k])
        gsum[...] = gx[x] + gx[NX] + gx[NX + 1] + gx[NX + 2]
        for k in (1, 2, 3):
            go_on(gsum, go.at[zl, :, lane(x)], gs.at[1, k - 1], gr.at[1, k - 1], "dp",
                  place(x, zl + k))
        keep = pltpu.make_async_copy(gsum, go.at[zl, :, lane(x)], gl)
        keep.start()
        keep.wait()

    def router_third():
        for k in (1, 2, 3):
            landed(go.at[lax.rem(zl + NL - k, NL), :, lane(x)], gr.at[1, k - 1])
        for k in (1, 2, 3):
            go_on(go.at[:, :, lane(x)], go.at[:, :, lane(x)], gs.at[2, k - 1], gr.at[2, k - 1],
                  "dp", place(x + k, zl))

    def router_last():
        for k in (1, 2, 3):
            landed(go.at[:, :, lane(x + NX - k)], gr.at[2, k - 1])

    acts_first(0)
    acts_first(1)
    pulls.first()
    part.reshape(2, rows, d)[0] = dot(hs[...], wts[2], ((1,), (1,))).astype(BF16)
    start_core(0)
    part.reshape(2, rows, d)[1] = (dot(dg[...], wts[0], ((1,), (1,)))
                                   + dot(du[...], wts[1], ((1,), (1,)))).astype(BF16)
    start_core(1)
    y_first()
    for dz in (0, 3, 1):
        slice_twin(dz)
    y_pass(2)
    y_plain(1)
    y_start(3)
    acts_second(0)
    acts_first(2)
    y_pass(1)
    y_plain(3)
    y_start(0)
    y_end(2)
    slice_twin(2)
    y_pass(3)
    y_plain(0)
    y_end(1)
    slice_in(1)
    weight_rows(0)
    across_first(0)
    acts_second(1)
    y_pass(0)
    y_end(3)
    pulls.second()
    acts_second(2)
    y_end(0)
    slice_in(0)
    weight_rows(1)
    pulls.third()
    z_second()
    across_first(1)
    pulls.last()
    router_first()
    weight_rows(2)
    router_second()
    across_first(2)
    across_second(0)
    across_second(1)
    across_second(2)
    router_third()
    to[0] = z_third(0)
    total = z_third(1)
    ours = lax.broadcasted_iota(jnp.int32, (8, rows), 0) + 8 * j
    pick = lax.broadcasted_iota(jnp.int32, (8, rows), 1) == ours
    for e in range(8):
        weight = jnp.sum(jnp.where(pick, lt[e : e + 1, :], 0.0), axis=1, keepdims=True)
        total = total + weight * rt[e : e + 1, :]
    to[1] = total
    write(to, to_hbm, 3)
    router_last()
    gout[...] = go[0] + go[1] + go[2] + go[3]
    write(gout, go_hbm, 4)
    for p in range(3):
        across_last(p)
    for copy in sent:
        copy.wait_send()
    for copy in writes:
        copy.wait()


def layer(tokens, cotangent, routes, router_t, w_gate, w_up, w_down):
    d = tokens.shape[1]
    f = w_gate.shape[1]
    rows = GROUP * 8
    n = d // (NX * NL)
    cols = d // NX
    dma = pltpu.SemaphoreType.DMA
    return pl.pallas_call(
        layer_kernel,
        out_shape=[
            jax.ShapeDtypeStruct((3, n, f), F32),
            jax.ShapeDtypeStruct((2, 8, d), F32),
            jax.ShapeDtypeStruct((8, d), F32),
        ],
        in_specs=[ANY] * 7,
        out_specs=[ANY] * 3,
        scratch_shapes=[
            pltpu.VMEM((8, d), BF16),
            pltpu.VMEM((8, d), BF16),
            pltpu.VMEM(routes.shape, jnp.int32),
            pltpu.VMEM(router_t.shape, F32),
            pltpu.VMEM((3, NL, n, f), BF16),
            pltpu.VMEM((NL, 8, d), F32),
            pltpu.VMEM((3, n, f), F32),
            pltpu.VMEM((2, 8, d), F32),
            pltpu.VMEM((8, d), F32),
            pltpu.VMEM((NY, NZ, 2, 8, d), BF16),
            pltpu.VMEM((NY, NZ, 2, 8, d), BF16),
            pltpu.VMEM((GROUP, 8, 128), F32),
            pltpu.VMEM((8, 128), F32),
            pltpu.VMEM((GROUP, 1, rows), F32),
            pltpu.VMEM((1, rows), F32),
            pltpu.VMEM((3, d, f), BF16),
            pltpu.VMEM((rows, f), F32),
            pltpu.VMEM((rows, f), F32),
            pltpu.VMEM((rows, f), F32),
            pltpu.VMEM((NX, 3, rows, f), BF16),
            pltpu.VMEM((8, rows), F32),
            pltpu.VMEM((2, NY, NZ, 2, 8, d), BF16),
            pltpu.VMEM((2, NY, NZ, 8, d), BF16),
            pltpu.VMEM((2, NY, NZ, 8, d), BF16),
            pltpu.VMEM((2, NZ, 8, d), BF16),
            pltpu.VMEM((2, 2, NZ, 8, d), BF16),
            pltpu.VMEM((2, NZ, 8, d), BF16),
            pltpu.VMEM((2, 8, d), BF16),
            pltpu.VMEM((2, 2, 8, d), BF16),
            pltpu.VMEM((2, 8, d), BF16),
            pltpu.VMEM((3, NL, n, f), BF16),
            pltpu.VMEM((2, NX - 1, NY, NZ, 2, 8, cols), BF16),
            pltpu.VMEM((3, n, f), BF16),
            pltpu.VMEM((NX + 3, 8, cols), F32),
            pltpu.VMEM((8, cols), F32),
            dma((4,)), dma((5,)), dma((3,)), dma((2, 31)), dma((2, GROUP)), dma((2,)),
            dma((31,)), dma((GROUP,)), dma((31,)), dma((GROUP,)), dma((2,)),
            dma((2, NY)), dma((2, NY)), dma((2, 3, NZ)), dma((2, 3, NZ)), dma((2, 3)), dma((2, 3)),
            dma((2, 3, NZ)), dma((2, 3, NZ)), dma((2, 3, NZ)), dma((2, 3, NZ)),
            dma((3, 2)), dma((3, 2)), dma((3, 2)), dma((3, 2)),
            dma((3, 3)), dma((3, 3)), dma((3,)), dma((3,)), dma((3, 3)), dma((3, 3)), dma,
        ],
        compiler_params=pltpu.CompilerParams(collective_id=0, has_side_effects=True),
        name="moe_layer",
    )(tokens, cotangent, routes, router_t, w_gate, w_up, w_down)


def finish_kernel(w, t, g, mo, to, go, o0, o1, o2):
    mo[...] = t[0].astype(BF16)
    to[...] = t[1].astype(BF16)
    go[...] = g[...]
    o0[...] = w[1]
    o1[...] = w[2]
    o2[...] = w[0]


def finish(w, t, g):
    grad = jax.ShapeDtypeStruct(w.shape[1:], F32)
    token = jax.ShapeDtypeStruct(t.shape[1:], BF16)
    return pl.pallas_call(
        finish_kernel,
        out_shape=[token, token, jax.ShapeDtypeStruct(g.shape, F32), grad, grad, grad],
        in_specs=[VMEM] * 3,
        out_specs=[VMEM] * 6,
        name="finish",
    )(w, t, g)


def local(tokens, routes, router, w_gate, w_up, w_down, cotangent):
    parts = layer(tokens, cotangent, routes, router.T, w_gate, w_up, w_down)
    mixed, grad_tokens, grad_router, grad_gate, grad_up, grad_down = finish(*parts)
    return (mixed, grad_tokens, grad_router.T, grad_gate, grad_up, grad_down)


def solution(mesh):
    return jax.shard_map(
        local,
        mesh=mesh,
        in_specs=(
            P(("dp", "expert"), None),
            P(("dp", "expert"), None),
            P(),
            P(None, "expert"),
            P(None, "expert"),
            P(None, "expert"),
            P(("dp", "expert"), None),
        ),
        out_specs=(
            P(("dp", "expert"), None),
            P(("dp", "expert"), None),
            P(),
            P("dp", "expert"),
            P("dp", "expert"),
            P("dp", "expert"),
        ),
        check_vma=False,
    )
```

time: 103 us -> 94.2 us (0.915)
  Pallas kernels: 100 us -> 93 us
    pallas_call x1, Pallas kernels: 98.3 us -> 91 us  [layer(): pl.pallas_call(layer_kernel, out_shape=[jax.ShapeDtypeStruct((3, n, f), F...]
where the time goes in v3:
time: 94.2 us; the launch traced here: 93.6 us
  Pallas kernels  93 us (99%)
    pallas_call x1, Pallas kernels, layer(): pl.pallas_call(layer_kernel, out_shape=[jax.ShapeDtypeStruct((3, n, f), F...  91 us
    pallas_call x1, Pallas kernels, finish(): pl.pallas_call(finish_kernel, out_shape=[token, token, jax.ShapeDtypeStru...  1.96 us

profile of v3, /device:TPU:1, one launch (start us, length us, event | category | flops | bytes accessed | tf_op | source)
XLA Modules:
  0.0 93.6 jit_solution(18288551585427951707)
XLA Ops:
  0.6 91.0 %moe_layer.1 = (f32[3,160,256]{2,1,0:T(8,128)}, f32[2,8,2560]{2,1,0:T(8,128)}, f32[8,2560]{1,0:T(8,128)}) custom-call(bf16[8,2560]{1,0:T(8,128)(2,1)} %x_hbm.1, bf16[8,2560]{1,0:T(8,128)(2,1)} %c_hbm.1, s32[8,6]{1,0:T(8,128)} %routes_hbm.1, f32[8,2560]{1,0:T(8,128)} %bitcast.2, bf16[2560,256]{1,0:T(8,128)(2,1)} %wg_hbm.1, bf16[2560,256]{1,0:T(8,128)(2,1)} %wu_hbm.1, ...), custom_call_target="tpu_custom_call" | custom-call | tf_op jit(solution)/shard_map/moe_layer/pallas_call | solution.py:542
  91.7 2.0 %finish.1 = (bf16[8,2560]{1,0:T(8,128)(2,1)}, bf16[8,2560]{1,0:T(8,128)(2,1)}, f32[8,2560]{1,0:T(8,128)}, f32[160,256]{1,0:T(8,128)}, f32[160,256]{1,0:T(8,128)}, /*index=5*/f32[160,256]{1,0:T(8,128)}) custom-call(f32[3,160,256]{2,1,0:T(8,128)} %get-tuple-element.15.w, f32[2,8,2560]{2,1,0:T(8,128)} %get-tuple-element.16.t, f32[8,2560]{1,0:T(8,128)} %get-tuple-element.17.g), custom_call_target="tpu_custom_call" | custom-call | tf_op jit(solution)/shard_map/finish/pallas_call | solution.py:611

commit v4 on v3

v4 whole, which is shorter than its diff:
```python
import jax
import jax.numpy as jnp
from jax import lax
from jax.experimental import pallas as pl
from jax.experimental.pallas import tpu as pltpu
from jax.sharding import PartitionSpec as P

NY = 4
NZ = 4
NX = 4
NL = 4
GROUP = 2 * NY * NZ
MESH = pl.DeviceIdType.MESH
VMEM = pl.BlockSpec(memory_space=pltpu.VMEM)
ANY = pl.BlockSpec(memory_space=pl.ANY)
F32 = jnp.float32
BF16 = jnp.bfloat16


def member(y, zh, core):
    return (lax.rem(y, NY) * NZ + lax.rem(zh, NZ)) * 2 + core


def dot(a, b, contract):
    return lax.dot_general(a, b, (contract, ((), ())), preferred_element_type=F32)


def thirds(a):
    one = a.astype(BF16).astype(F32)
    two = (a - one).astype(BF16).astype(F32)
    return jnp.concatenate([one, two, a - one - two], axis=0).astype(BF16)


def regroup(a):
    n = a.shape[0] // 3
    return a[:n] + a[n : 2 * n] + a[2 * n :]


def layer_kernel(x_hbm, c_hbm, routes_hbm, rt_hbm, wg_hbm, wu_hbm, wd_hbm,
                 wo_hbm, to_hbm, go_hbm,
                 x_ref, c_ref, routes_ref, rt, zo, gz, wo, to, gout,
                 xg, cg, mg, m_ref, pg, prow, wts, gate_pre, up_pre, pull, acts, lt,
                 part, cbuf, q, s1, fy, r, s1z, fz, r2,
                 dw, slices, aid, gx, gsum, gtot,
                 isem, osem, wsem, as_, ar, al, ms, mr, ps, pr, ml, cs, cr, ys, yr, zs, zr,
                 es, er, ts, tr, xs, xr, vr, us, ur, hr, gs, gr):
    j = lax.axis_index("expert")
    core = lax.rem(j, 2)
    zh = lax.rem(lax.div(j, 2), NZ)
    y = lax.div(j, 2 * NZ)
    dev = lax.axis_index("dp")
    x, zl = lax.div(dev, NL), lax.rem(dev, NL)
    d = x_ref.shape[1]
    rows = GROUP * 8

    def place(xx, zz):
        return lax.rem(xx, NX) * NL + lax.rem(zz, NL)

    def at(dy, dz):
        return member(y + dy, zh + dz, core)

    twin = member(y, zh, 1 - core)
    z_up, z_down, y_up, y_down = at(0, 1), at(0, 3), at(1, 0), at(3, 0)
    x_up, x_down = place(x + 1, zl), place(x + 3, zl)

    reads = [pltpu.make_async_copy(src, dst, isem.at[i])
             for i, (src, dst) in enumerate(((x_hbm, x_ref), (c_hbm, c_ref),
                                             (routes_hbm, routes_ref), (rt_hbm, rt)))]
    for copy in reads:
        copy.start()
    loads = [pltpu.make_async_copy(w, wts.at[i], wsem.at[i])
             for i, w in enumerate((wg_hbm, wu_hbm, wd_hbm))]
    for copy in loads:
        copy.start()

    barrier = pltpu.get_barrier_semaphore()
    near = [at(0, 1), at(0, 2), at(0, 3), at(1, 0), at(2, 0), at(3, 0), twin]
    wide = [place(x + k, zl) for k in (1, 2, 3)] + [place(x, zl + k) for k in (1, 2, 3)]
    for peer in near:
        pl.semaphore_signal(barrier, inc=1, device_id={"expert": peer}, device_id_type=MESH)
    for peer in wide:
        pl.semaphore_signal(barrier, inc=1, device_id={"dp": peer}, device_id_type=MESH)
    for copy in reads:
        copy.wait()
    lanes = lax.broadcasted_iota(jnp.int32, m_ref.shape, 1)
    m_ref[...] = sum((routes_ref[:, k : k + 1] == lanes).astype(F32)
                     for k in range(routes_ref.shape[1]))
    pl.semaphore_wait(barrier, len(near) + len(wide))


    def remote(src, dst, send_sem, recv_sem, axis, target):
        return pltpu.make_async_remote_copy(
            src_ref=src, dst_ref=dst, send_sem=send_sem, recv_sem=recv_sem,
            device_id={axis: target}, device_id_type=MESH,
        )

    def go_on(*args):
        remote(*args).start()

    def landed(ref, sem):
        remote(ref, ref, sem, sem, "expert", twin).wait_recv()

    def gone(ref, sem):
        remote(ref, ref, sem, sem, "expert", twin).wait_send()

    ins, outs = (x_ref, c_ref), (xg, cg)
    three = cbuf.at[0, 0, pl.ds(0, 3)]

    def send(a, dy, dz, target, sem, own=False):
        block = lax.rem(y + dy, NY), lax.rem(zh + dz, NZ), core
        go_on(ins[a] if own else outs[a].at[block], outs[a].at[block],
              as_.at[a], ar.at[a, sem], "expert", target)

    def arrive_twin(a):
        landed(outs[a].at[:, :, 1 - core], ar.at[a, 7])

    def spread(a, dz, own=False):
        for target in (y_up, y_down, at(2, 0)):
            send(a, 0, dz, target, 3 + dz, own)
        send(a, 0, dz, twin, 7, own)

    def from_z(a, dz):
        landed(outs[a].at[y, lax.rem(zh + dz, NZ), core], ar.at[a, dz - 1])
        spread(a, dz)

    def from_y(a, dz):
        landed(three, ar.at[a, 3 + dz])
        for dy in (3, 1, 2):
            send(a, dy, dz, twin, 7)

    cols = d // NX

    def lane(xx):
        return pl.ds(pl.multiple_of(lax.rem(xx, NX) * cols, cols), cols)

    def slice_out(a, dz):
        zz = lax.rem(zh + dz, NZ)
        for k in (2, 1, 3):
            go_on(outs[a].at[:, zz, core, :, lane(x + k)], slices.at[a, k - 1, :, zz, core],
                  es, er.at[a], "dp", place(x + k, zl))

    def slice_twin(a):
        ref = slices.at[a, :, :, :, core]
        landed(ref, er.at[a])
        go_on(ref, ref, ts, tr.at[a], "expert", twin)

    def slice_in(a):
        landed(slices.at[a, :, :, :, 1 - core], tr.at[a])

    class Small:
        def __init__(self, src, out, ssem, rsem, local):
            self.src, self.out, self.ssem, self.rsem = src, out, ssem, rsem
            self.keep = pltpu.make_async_copy(src, out.at[j], local)

        def send(self, block, target, sem, own=False):
            go_on(self.src if own else self.out.at[block], self.out.at[block],
                  self.ssem, self.rsem.at[sem], "expert", target)

        def spread(self, dz, own=False):
            for target in (y_up, y_down, at(2, 0)):
                self.send(at(0, dz), target, 3 + dz, own)
            self.send(at(0, dz), twin, 7, own)

        def first(self):
            for k in (1, 2, 3):
                self.send(j, at(0, k), 3 - k, True)
            self.spread(0, True)
            self.keep.start()

        def second(self):
            for dz in (1, 3, 2):
                landed(self.out.at[at(0, dz)], self.rsem.at[dz - 1])
                self.spread(dz)

        def third(self):
            for dz in (0, 1, 3, 2):
                landed(self.out.at[pl.ds(0, 3)], self.rsem.at[3 + dz])
                for dy in (1, 3, 2):
                    self.send(at(dy, dz), twin, 7)

        def last(self):
            self.keep.wait()
            landed(self.out.at[pl.ds(0, NY * NZ)], self.rsem.at[7])

        def done(self):
            gone(self.out.at[pl.ds(0, GROUP - 1)], self.ssem)

    marks = Small(m_ref, mg, ms, mr, ml.at[0])
    pulls = Small(prow, pg, ps, pr, ml.at[1])

    for a in range(2):
        for k in (1, 3, 2):
            send(a, 0, 0, at(0, k), 3 - k, True)
        if a == 0:
            marks.first()
    for a in range(2):
        spread(a, 0, True)
    held = [pltpu.make_async_copy(ins[a], outs[a].at[y, zh, core], al.at[a]) for a in range(2)]
    for copy in held:
        copy.start()
    def all_y(a, dz):
        from_y(a, dz)
        slice_out(a, dz)

    for copy in loads + held:
        copy.wait()
    all_y(0, 0)
    for dz in (3, 1, 2):
        from_z(0, dz)
    marks.second()
    all_y(1, 0)
    for dz in (3, 1):
        from_z(1, dz)
    for dz in (3, 1, 2):
        all_y(0, dz)
    marks.third()
    from_z(1, 2)
    arrive_twin(0)

    xv, cv = xg.reshape(rows, d), cg.reshape(rows, d)
    gate_pre[...] = dot(xv[...], wts[0], ((1,), (0,)))
    up_pre[...] = dot(xv[...], wts[1], ((1,), (0,)))
    logits = regroup(dot(thirds(rt[...]), xv[...], ((1,), (1,))))
    affinity = jax.nn.sigmoid(logits)
    for dz in (3, 1):
        all_y(1, dz)
    marks.last()
    mask = jnp.transpose(mg.reshape(rows, 128)[...])[:8]
    denominator = jnp.sum(affinity * mask, axis=0, keepdims=True)
    gates = mask * affinity / denominator
    wide_gates = jnp.transpose(jnp.concatenate([gates, jnp.zeros((120, rows), F32)], axis=0))
    mine = lax.broadcasted_iota(jnp.int32, wide_gates.shape, 1) == lax.div(j, 4)
    gate = jnp.sum(jnp.where(mine, wide_gates, 0.0), axis=1, keepdims=True)
    hs, dg, du = acts.at[0, 0], acts.at[0, 1], acts.at[0, 2]
    hs[...] = (gate * (gate_pre[...] * jax.nn.sigmoid(gate_pre[...]) * up_pre[...])).astype(BF16)

    def hidden_back():
        pull[...] = dot(cv[...], wts[2], ((1,), (0,)))
        sigma = jax.nn.sigmoid(gate_pre[...])
        silu = gate_pre[...] * sigma
        hidden = silu * up_pre[...]
        prow[...] = jnp.sum(jnp.transpose(hidden * pull[...]), axis=0, keepdims=True)
        hidden_grad = gate * pull[...]
        dg[...] = (hidden_grad * up_pre[...] * sigma
                   * (1.0 + gate_pre[...] * (1.0 - sigma))).astype(BF16)
        du[...] = (hidden_grad * silu).astype(BF16)

    half = rows // 2
    ends = pl.ds(0, half), pl.ds(half, half)

    def acts_first(p):
        go_on(acts.at[0, p], acts.at[1, p], xs, xr.at[p, 0], "dp", x_up)
        go_on(acts.at[0, p], acts.at[3, p], xs, xr.at[p, 1], "dp", x_down)

    def acts_second(p):
        for h in range(2):
            landed(acts.at[(1, 3)[h], p], xr.at[p, h])
            go_on(acts.at[(1, 3)[h], p, ends[h]], acts.at[2, p, ends[h]], xs,
                  vr.at[p], "dp", (x_up, x_down)[h])

    def weight_rows(p):
        landed(acts.at[2, p], vr.at[p])
        a = 0 if p else 1
        value = dot((cv, xv)[p > 0][:, lane(x)], acts[0, p], ((0,), (0,)))
        for k in (1, 2, 3):
            other = slices.at[a, k - 1].reshape(rows, cols)
            value = value + dot(other[...], acts[k, p], ((0,), (0,)))
        dw[p] = value.astype(BF16).reshape(dw.shape[1:])

    writes = []

    def write(src, dst, i):
        copy = pltpu.make_async_copy(src, dst, osem.at[i])
        copy.start()
        writes.append(copy)

    is_end = jnp.logical_or(zl == 0, zl == NL - 1)

    def hop(p, k, to_aid):
        shard = dw.at[p, lax.rem(zl + k, NL)]
        if to_aid:
            return remote(shard, aid.at[p], us, hr.at[p], "dp", place(x, zl + NL - k))
        return remote(shard, zo.at[p, k], us, ur.at[p, k - 1], "dp",
                      place(x, zl + k))

    def across_first(p):
        for k, end in ((3, 0), (1, NL - 1)):
            @pl.when(zl == end)
            def _():
                hop(p, k, True).start()

            @pl.when(zl != end)
            def _():
                hop(p, k, False).start()

        @pl.when(is_end)
        def _():
            hop(p, 2, False).start()

        zo[p, 0] = dw[p, zl]

        @pl.when(zl == 0)
        def _():
            zo[p, 1] = jnp.zeros(zo.shape[2:], BF16)

        @pl.when(zl == NL - 1)
        def _():
            zo[p, 3] = jnp.zeros(zo.shape[2:], BF16)

    def across_second(p):
        @pl.when(jnp.logical_not(is_end))
        def _():
            landed(aid.at[p], hr.at[p])
            aid[p] = (dw[p, lax.rem(zl + 2, NL)].astype(F32) + aid[p].astype(F32)).astype(BF16)
            remote(aid.at[p], zo.at[p, 2], us, ur.at[p, 1], "dp",
                   place(x, zl + 2)).start()

    def across_last(p):
        landed(zo.at[p, 2], ur.at[p, 1])
        for k, none in ((3, NL - 1), (1, 0)):
            @pl.when(zl != none)
            def _():
                landed(zo.at[p, k], ur.at[p, k - 1])

        wo[p] = (zo[p, 0].astype(F32) + zo[p, 1].astype(F32)
                 + zo[p, 2].astype(F32) + zo[p, 3].astype(F32))
        write(wo.at[p], wo_hbm.at[p], p)

    def start_core(a):
        for dy in (2, 1, 3, 0):
            yy = lax.rem(y + dy, NY)
            go_on(part.at[a, yy, :, 1 - core], cbuf.at[a, yy], cs, cr.at[a, yy],
                  "expert", twin)

    def add_core(a, dy):
        yy = lax.rem(y + dy, NY)
        landed(cbuf.at[a, yy], cr.at[a, yy])

        @pl.loop(0, NZ)
        def _(k):
            q[a, yy, k] = (part[a, yy, k, core].astype(F32)
                           + cbuf[a, yy, k].astype(F32)).astype(BF16)

    y1, y2, y3 = lax.rem(y + 1, NY), lax.rem(y + 2, NY), lax.rem(y + 3, NY)

    def row(k):
        return lax.rem(zh + k, NZ)

    def y_start(a, k):
        zz = row(k)
        go_on(q.at[a, y2, zz], s1.at[a, zz], ys, yr.at[a, 0, k], "expert",
              (y_up, y_down)[a])

    def y_first(a):
        for dy in (2, 1, 3):
            add_core(a, dy)
        y_start(a, 2)
        y_start(a, 1)
        for k in (2, 1, 3, 0):
            go_on(q.at[a, (y3, y1)[a], row(k)], fy.at[a, 1 - a, row(k)], ys,
                  yr.at[a, 1, k], "expert", (y_down, y_up)[a])
        add_core(a, 0)

    def y_pass(a, k):
        zz = row(k)
        landed(s1.at[a, zz], yr.at[a, 0, k])
        s1[a, zz] = (q[a, (y1, y3)[a], zz].astype(F32) + s1[a, zz].astype(F32)).astype(BF16)
        go_on(s1.at[a, zz], fy.at[a, a, zz], ys, yr.at[a, 1, k], "expert",
              (y_up, y_down)[a])

    h1, h2, h3 = lax.rem(zh + 1, NZ), lax.rem(zh + 2, NZ), lax.rem(zh + 3, NZ)

    def y_end(a, k):
        zz = row(k)
        landed(fy.at[a, :, zz], yr.at[a, 1, k])
        r[a, zz] = (q[a, y, zz].astype(F32) + fy[a, 0, zz].astype(F32)
                    + fy[a, 1, zz].astype(F32)).astype(BF16)
        if k == 2:
            go_on(r.at[a, zz], s1z.at[a], zs, zr.at[a, 0], "expert", (z_up, z_down)[a])
        if k == (3, 1)[a]:
            go_on(r.at[a, zz], fz.at[a, 1 - a], zs, zr.at[a, 1], "expert",
                  (z_down, z_up)[a])

    def z_second(a):
        landed(s1z.at[a], zr.at[a, 0])
        r2[a] = (r[a, (h1, h3)[a]].astype(F32) + s1z[a].astype(F32)).astype(BF16)
        go_on(r2.at[a], fz.at[a, a], zs, zr.at[a, 1], "expert",
              (z_up, z_down)[a])

    def z_third(a):
        landed(fz.at[a], zr.at[a, 1])
        return r[a, zh].astype(F32) + fz[a, 0].astype(F32) + fz[a, 1].astype(F32)

    def router_first():
        sums = []
        for e in range(8):
            sums.append(pg[4 * e] + pg[4 * e + 1] + pg[4 * e + 2] + pg[4 * e + 3])
        full = jnp.concatenate(sums, axis=0)
        mean = jnp.sum(gates * full, axis=0, keepdims=True)
        lt[...] = mask * (full - mean) / denominator * affinity * (1.0 - affinity)
        value = regroup(dot(thirds(lt[...]), xv[...], ((1,), (0,))))
        for k in range(NX):
            gx[k] = value[:, k * cols : (k + 1) * cols]
        for k in (1, 2, 3):
            go_on(gx.at[lax.rem(x + k, NX)], gx.at[NX + k - 1], gs.at[0],
                  gr.at[0], "dp", place(x + k, zl))

    def router_second():
        landed(gx.at[pl.ds(NX, 3)], gr.at[0])
        gsum[...] = gx[x] + gx[NX] + gx[NX + 1] + gx[NX + 2]
        for k in (1, 2, 3):
            go_on(gsum, gz.at[k - 1], gs.at[1], gr.at[1], "dp", place(x, zl + k))

    def router_third():
        landed(gz, gr.at[1])
        gtot[...] = gsum[...] + gz[0] + gz[1] + gz[2]
        for k in (1, 2, 3):
            go_on(gtot, gout.at[:, lane(x)], gs.at[2], gr.at[2], "dp",
                  place(x + k, zl))
        gout[:, lane(x)] = gtot[...]

    def router_last():
        landed(gz, gr.at[2])

    acts_first(0)
    part.reshape(2, rows, d)[0] = dot(hs[...], wts[2], ((1,), (1,))).astype(BF16)
    start_core(0)
    all_y(1, 2)
    y_first(0)
    y_pass(0, 2)
    y_start(0, 3)
    acts_second(0)
    y_pass(0, 1)
    y_start(0, 0)
    arrive_twin(1)
    hidden_back()
    acts_first(1)
    acts_first(2)
    pulls.first()
    y_pass(0, 3)
    y_end(0, 2)
    part.reshape(2, rows, d)[1] = (dot(dg[...], wts[0], ((1,), (1,)))
                                   + dot(du[...], wts[1], ((1,), (1,)))).astype(BF16)
    start_core(1)
    y_pass(0, 0)
    y_end(0, 1)
    y_first(1)
    slice_twin(1)
    y_end(0, 3)
    slice_in(1)
    weight_rows(0)
    across_first(0)
    y_pass(1, 2)
    y_start(1, 3)
    y_end(0, 0)
    slice_twin(0)
    acts_second(1)
    y_pass(1, 1)
    y_start(1, 0)
    z_second(0)
    y_end(1, 2)
    y_pass(1, 3)
    acts_second(2)
    pulls.second()
    y_pass(1, 0)
    y_end(1, 1)
    slice_in(0)
    weight_rows(1)
    across_first(1)
    y_end(1, 3)
    pulls.third()
    across_second(0)
    weight_rows(2)
    across_first(2)
    pulls.last()
    router_first()
    y_end(1, 0)
    z_second(1)
    router_second()
    across_second(1)
    across_second(2)
    router_third()
    to[0] = z_third(0)
    total = z_third(1)
    ours = lax.broadcasted_iota(jnp.int32, (8, rows), 0) + 8 * j
    pick = lax.broadcasted_iota(jnp.int32, (8, rows), 1) == ours
    for e in range(8):
        weight = jnp.sum(jnp.where(pick, lt[e : e + 1, :], 0.0), axis=1, keepdims=True)
        total = total + weight * rt[e : e + 1, :]
    to[1] = total
    write(to, to_hbm, 3)
    router_last()
    write(gout, go_hbm, 4)
    for p in range(3):
        across_last(p)
    for a in range(2):
        gone(outs[a].reshape(GROUP, 8, d).at[pl.ds(0, GROUP - 1)], as_.at[a])
    marks.done()
    pulls.done()
    gone(slices.at[:, :, :, :, 0], es)
    gone(slices.at[:, :, :, :, 0], ts)
    gone(cbuf, cs)
    gone(cbuf.at[:, pl.ds(0, 3)], ys)
    gone(cbuf.at[:, 0, pl.ds(0, 3)], zs)
    gone(acts.at[pl.ds(0, 3)], xs)
    gone(zo.at[:, pl.ds(0, 3)], us)
    for i in range(3):
        gone(gz, gs.at[i])
    for copy in writes:
        copy.wait()


def layer(tokens, cotangent, routes, router_t, w_gate, w_up, w_down):
    d = tokens.shape[1]
    f = w_gate.shape[1]
    rows = GROUP * 8
    n = d // (NX * NL)
    cols = d // NX
    dma = pltpu.SemaphoreType.DMA
    return pl.pallas_call(
        layer_kernel,
        out_shape=[
            jax.ShapeDtypeStruct((3, n, f), F32),
            jax.ShapeDtypeStruct((2, 8, d), F32),
            jax.ShapeDtypeStruct((8, d), F32),
        ],
        in_specs=[ANY] * 7,
        out_specs=[ANY] * 3,
        scratch_shapes=[
            pltpu.VMEM((8, d), BF16),
            pltpu.VMEM((8, d), BF16),
            pltpu.VMEM(routes.shape, jnp.int32),
            pltpu.VMEM(router_t.shape, F32),
            pltpu.VMEM((3, NL, n, f), BF16),
            pltpu.VMEM((NL - 1, 8, cols), F32),
            pltpu.VMEM((3, n, f), F32),
            pltpu.VMEM((2, 8, d), F32),
            pltpu.VMEM((8, d), F32),
            pltpu.VMEM((NY, NZ, 2, 8, d), BF16),
            pltpu.VMEM((NY, NZ, 2, 8, d), BF16),
            pltpu.VMEM((GROUP, 8, 128), F32),
            pltpu.VMEM((8, 128), F32),
            pltpu.VMEM((GROUP, 1, rows), F32),
            pltpu.VMEM((1, rows), F32),
            pltpu.VMEM((3, d, f), BF16),
            pltpu.VMEM((rows, f), F32),
            pltpu.VMEM((rows, f), F32),
            pltpu.VMEM((rows, f), F32),
            pltpu.VMEM((NX, 3, rows, f), BF16),
            pltpu.VMEM((8, rows), F32),
            pltpu.VMEM((2, NY, NZ, 2, 8, d), BF16),
            pltpu.VMEM((2, NY, NZ, 8, d), BF16),
            pltpu.VMEM((2, NY, NZ, 8, d), BF16),
            pltpu.VMEM((2, NZ, 8, d), BF16),
            pltpu.VMEM((2, 2, NZ, 8, d), BF16),
            pltpu.VMEM((2, NZ, 8, d), BF16),
            pltpu.VMEM((2, 8, d), BF16),
            pltpu.VMEM((2, 2, 8, d), BF16),
            pltpu.VMEM((2, 8, d), BF16),
            pltpu.VMEM((3, NL, n, f), BF16),
            pltpu.VMEM((2, NX - 1, NY, NZ, 2, 8, cols), BF16),
            pltpu.VMEM((3, n, f), BF16),
            pltpu.VMEM((NX + 3, 8, cols), F32),
            pltpu.VMEM((8, cols), F32),
            pltpu.VMEM((8, cols), F32),
            dma((4,)), dma((5,)), dma((3,)), dma((2,)), dma((2, 8)), dma((2,)),
            dma, dma((8,)), dma, dma((8,)), dma((2,)),
            dma, dma((2, NY)), dma, dma((2, 2, NZ)), dma, dma((2, 2)),
            dma, dma((2,)), dma, dma((2,)),
            dma, dma((3, 2)), dma((3,)), dma, dma((3, 3)), dma((3,)), dma((3,)), dma((3,)),
        ],
        compiler_params=pltpu.CompilerParams(collective_id=0, has_side_effects=True),
        name="moe_layer",
    )(tokens, cotangent, routes, router_t, w_gate, w_up, w_down)


def finish_kernel(w, t, g, mo, to, go, o0, o1, o2):
    mo[...] = t[0].astype(BF16)
    to[...] = t[1].astype(BF16)
    go[...] = g[...]
    o0[...] = w[1]
    o1[...] = w[2]
    o2[...] = w[0]


def finish(w, t, g):
    grad = jax.ShapeDtypeStruct(w.shape[1:], F32)
    token = jax.ShapeDtypeStruct(t.shape[1:], BF16)
    return pl.pallas_call(
        finish_kernel,
        out_shape=[token, token, jax.ShapeDtypeStruct(g.shape, F32), grad, grad, grad],
        in_specs=[VMEM] * 3,
        out_specs=[VMEM] * 6,
        name="finish",
    )(w, t, g)


def local(tokens, routes, router, w_gate, w_up, w_down, cotangent):
    parts = layer(tokens, cotangent, routes, router.T, w_gate, w_up, w_down)
    mixed, grad_tokens, grad_router, grad_gate, grad_up, grad_down = finish(*parts)
    return (mixed, grad_tokens, grad_router.T, grad_gate, grad_up, grad_down)


def solution(mesh):
    return jax.shard_map(
        local,
        mesh=mesh,
        in_specs=(
            P(("dp", "expert"), None),
            P(("dp", "expert"), None),
            P(),
            P(None, "expert"),
            P(None, "expert"),
            P(None, "expert"),
            P(("dp", "expert"), None),
        ),
        out_specs=(
            P(("dp", "expert"), None),
            P(("dp", "expert"), None),
            P(),
            P("dp", "expert"),
            P("dp", "expert"),
            P("dp", "expert"),
        ),
        check_vma=False,
    )
```

time: 94.2 us -> 90.3 us (0.959)
  Pallas kernels: 93 us -> 89 us
    pallas_call x1, Pallas kernels: 91 us -> 87 us  [layer(): pl.pallas_call(layer_kernel, out_shape=[jax.ShapeDtypeStruct((3, n, f), F...]
where the time goes in v4:
time: 90.3 us; the launch traced here: 89.6 us
  Pallas kernels  89 us (99%)
    pallas_call x1, Pallas kernels, layer(): pl.pallas_call(layer_kernel, out_shape=[jax.ShapeDtypeStruct((3, n, f), F...  87 us
    pallas_call x1, Pallas kernels, finish(): pl.pallas_call(finish_kernel, out_shape=[token, token, jax.ShapeDtypeStru...  1.96 us

profile of v4, /device:TPU:1, one launch (start us, length us, event | category | flops | bytes accessed | tf_op | source)
XLA Modules:
  0.0 89.6 jit_solution(6863069252758493352)
XLA Ops:
  0.6 87.0 %moe_layer.1 = (f32[3,160,256]{2,1,0:T(8,128)}, f32[2,8,2560]{2,1,0:T(8,128)}, f32[8,2560]{1,0:T(8,128)}) custom-call(bf16[8,2560]{1,0:T(8,128)(2,1)} %x_hbm.1, bf16[8,2560]{1,0:T(8,128)(2,1)} %c_hbm.1, s32[8,6]{1,0:T(8,128)} %routes_hbm.1, f32[8,2560]{1,0:T(8,128)} %bitcast.2, bf16[2560,256]{1,0:T(8,128)(2,1)} %wg_hbm.1, bf16[2560,256]{1,0:T(8,128)(2,1)} %wu_hbm.1, ...), custom_call_target="tpu_custom_call" | custom-call | tf_op jit(solution)/shard_map/moe_layer/pallas_call | solution.py:520
  87.6 2.0 %finish.1 = (bf16[8,2560]{1,0:T(8,128)(2,1)}, bf16[8,2560]{1,0:T(8,128)(2,1)}, f32[8,2560]{1,0:T(8,128)}, f32[160,256]{1,0:T(8,128)}, f32[160,256]{1,0:T(8,128)}, /*index=5*/f32[160,256]{1,0:T(8,128)}) custom-call(f32[3,160,256]{2,1,0:T(8,128)} %get-tuple-element.15.w, f32[2,8,2560]{2,1,0:T(8,128)} %get-tuple-element.16.t, f32[8,2560]{1,0:T(8,128)} %get-tuple-element.17.g), custom_call_target="tpu_custom_call" | custom-call | tf_op jit(solution)/shard_map/finish/pallas_call | solution.py:589

commit v5 on v4

--- a/solution.py
+++ b/solution.py
@@ -74,7 +74,7 @@
         copy.start()
 
     barrier = pltpu.get_barrier_semaphore()
-    near = [at(0, 1), at(0, 2), at(0, 3), at(1, 0), at(2, 0), at(3, 0), twin]
+    near = [at(0, 1), at(0, 3), at(1, 0), at(2, 0), at(3, 0), twin]
     wide = [place(x + k, zl) for k in (1, 2, 3)] + [place(x, zl + k) for k in (1, 2, 3)]
     for peer in near:
         pl.semaphore_signal(barrier, inc=1, device_id={"expert": peer}, device_id_type=MESH)
@@ -120,7 +120,11 @@
         send(a, 0, dz, twin, 7, own)
 
     def from_z(a, dz):
-        landed(outs[a].at[y, lax.rem(zh + dz, NZ), core], ar.at[a, dz - 1])
+        zz = lax.rem(zh + dz, NZ)
+        landed(outs[a].at[y, zz, core], ar.at[a, dz - 1])
+        if dz != 2:
+            ref = outs[a].at[y, zz, core, :, pl.ds((dz - 1) // 2 * (d // 2), d // 2)]
+            go_on(ref, ref, as_.at[a], ar.at[a, 1], "expert", z_up if dz == 3 else z_down)
         spread(a, dz)
 
     def from_y(a, dz):
@@ -162,14 +166,16 @@
             self.send(at(0, dz), twin, 7, own)
 
         def first(self):
-            for k in (1, 2, 3):
+            for k in (1, 3):
                 self.send(j, at(0, k), 3 - k, True)
             self.spread(0, True)
             self.keep.start()
 
-        def second(self):
-            for dz in (1, 3, 2):
+        def second(self, *sides):
+            for dz in sides:
                 landed(self.out.at[at(0, dz)], self.rsem.at[dz - 1])
+                if dz == 3:
+                    self.send(at(0, dz), z_up, 1)
                 self.spread(dz)
 
         def third(self):
@@ -189,7 +195,7 @@
     pulls = Small(prow, pg, ps, pr, ml.at[1])
 
     for a in range(2):
-        for k in (1, 3, 2):
+        for k in (1, 3):
             send(a, 0, 0, at(0, k), 3 - k, True)
         if a == 0:
             marks.first()
@@ -205,14 +211,17 @@
     for copy in loads + held:
         copy.wait()
     all_y(0, 0)
-    for dz in (3, 1, 2):
+    for dz in (3, 1):
         from_z(0, dz)
-    marks.second()
+    marks.second(3, 1)
+    from_z(0, 2)
     all_y(1, 0)
     for dz in (3, 1):
         from_z(1, dz)
-    for dz in (3, 1, 2):
+    for dz in (3, 1):
         all_y(0, dz)
+    marks.second(2)
+    all_y(0, 2)
     marks.third()
     from_z(1, 2)
     arrive_twin(0)
@@ -445,6 +454,7 @@
     y_pass(0, 0)
     y_end(0, 1)
     y_first(1)
+    pulls.second(3, 1)
     slice_twin(1)
     y_end(0, 3)
     slice_in(1)
@@ -459,24 +469,24 @@
     y_start(1, 0)
     z_second(0)
     y_end(1, 2)
+    pulls.second(2)
     y_pass(1, 3)
     acts_second(2)
-    pulls.second()
     y_pass(1, 0)
     y_end(1, 1)
+    pulls.third()
     slice_in(0)
     weight_rows(1)
     across_first(1)
     y_end(1, 3)
-    pulls.third()
+    pulls.last()
+    router_first()
     across_second(0)
     weight_rows(2)
+    router_second()
     across_first(2)
-    pulls.last()
-    router_first()
     y_end(1, 0)
     z_second(1)
-    router_second()
     across_second(1)
     across_second(2)
     router_third()

time: 90.3 us -> 89.4 us (0.990)
  no operation moved by 1% of the time
where the time goes in v5:
time: 89.4 us; the launch traced here: 89.3 us
  Pallas kernels  88.6 us (99%)
    pallas_call x1, Pallas kernels, layer(): pl.pallas_call(layer_kernel, out_shape=[jax.ShapeDtypeStruct((3, n, f), F...  86.6 us
    pallas_call x1, Pallas kernels, finish(): pl.pallas_call(finish_kernel, out_shape=[token, token, jax.ShapeDtypeStru...  1.96 us

profile of v5, /device:TPU:1, one launch (start us, length us, event | category | flops | bytes accessed | tf_op | source)
XLA Modules:
  0.0 89.3 jit_solution(11909905740107694803)
XLA Ops:
  0.6 86.6 %moe_layer.1 = (f32[3,160,256]{2,1,0:T(8,128)}, f32[2,8,2560]{2,1,0:T(8,128)}, f32[8,2560]{1,0:T(8,128)}) custom-call(bf16[8,2560]{1,0:T(8,128)(2,1)} %x_hbm.1, bf16[8,2560]{1,0:T(8,128)(2,1)} %c_hbm.1, s32[8,6]{1,0:T(8,128)} %routes_hbm.1, f32[8,2560]{1,0:T(8,128)} %bitcast.2, bf16[2560,256]{1,0:T(8,128)(2,1)} %wg_hbm.1, bf16[2560,256]{1,0:T(8,128)(2,1)} %wu_hbm.1, ...), custom_call_target="tpu_custom_call" | custom-call | tf_op jit(solution)/shard_map/moe_layer/pallas_call | solution.py:530
  87.3 2.0 %finish.1 = (bf16[8,2560]{1,0:T(8,128)(2,1)}, bf16[8,2560]{1,0:T(8,128)(2,1)}, f32[8,2560]{1,0:T(8,128)}, f32[160,256]{1,0:T(8,128)}, f32[160,256]{1,0:T(8,128)}, /*index=5*/f32[160,256]{1,0:T(8,128)}) custom-call(f32[3,160,256]{2,1,0:T(8,128)} %get-tuple-element.15.w, f32[2,8,2560]{2,1,0:T(8,128)} %get-tuple-element.16.t, f32[8,2560]{1,0:T(8,128)} %get-tuple-element.17.g), custom_call_target="tpu_custom_call" | custom-call | tf_op jit(solution)/shard_map/finish/pallas_call | solution.py:599

commit v6 on v5

--- a/solution.py
+++ b/solution.py
@@ -293,6 +293,11 @@
                       place(x, zl + k))
 
     def across_first(p):
+        zo[p, 0] = dw[p, zl]
+        if p == 2:
+            for k in (2, 1, 3):
+                hop(p, k, False).start()
+            return
         for k, end in ((3, 0), (1, NL - 1)):
             @pl.when(zl == end)
             def _():
@@ -305,8 +310,6 @@
         @pl.when(is_end)
         def _():
             hop(p, 2, False).start()
-
-        zo[p, 0] = dw[p, zl]
 
         @pl.when(zl == 0)
         def _():
@@ -327,7 +330,7 @@
     def across_last(p):
         landed(zo.at[p, 2], ur.at[p, 1])
         for k, none in ((3, NL - 1), (1, 0)):
-            @pl.when(zl != none)
+            @pl.when(zl != (none if p < 2 else NL))
             def _():
                 landed(zo.at[p, k], ur.at[p, k - 1])
 
@@ -488,7 +491,6 @@
     y_end(1, 0)
     z_second(1)
     across_second(1)
-    across_second(2)
     router_third()
     to[0] = z_third(0)
     total = z_third(1)

time: 89.4 us -> 91.2 us (1.020)
  Pallas kernels: 88.6 us -> 90.4 us
    pallas_call x1, Pallas kernels: 86.6 us -> 88.5 us  [layer(): pl.pallas_call(layer_kernel, out_shape=[jax.ShapeDtypeStruct((3, n, f), F...]
where the time goes in v6:
time: 91.2 us; the launch traced here: 91.1 us
  Pallas kernels  90.4 us (99%)
    pallas_call x1, Pallas kernels, layer(): pl.pallas_call(layer_kernel, out_shape=[jax.ShapeDtypeStruct((3, n, f), F...  88.5 us
    pallas_call x1, Pallas kernels, finish(): pl.pallas_call(finish_kernel, out_shape=[token, token, jax.ShapeDtypeStru...  1.96 us

profile of v6, /device:TPU:1, one launch (start us, length us, event | category | flops | bytes accessed | tf_op | source)
XLA Modules:
  0.0 91.1 jit_solution(8842168134252890494)
XLA Ops:
  0.6 88.5 %moe_layer.1 = (f32[3,160,256]{2,1,0:T(8,128)}, f32[2,8,2560]{2,1,0:T(8,128)}, f32[8,2560]{1,0:T(8,128)}) custom-call(bf16[8,2560]{1,0:T(8,128)(2,1)} %x_hbm.1, bf16[8,2560]{1,0:T(8,128)(2,1)} %c_hbm.1, s32[8,6]{1,0:T(8,128)} %routes_hbm.1, f32[8,2560]{1,0:T(8,128)} %bitcast.2, bf16[2560,256]{1,0:T(8,128)(2,1)} %wg_hbm.1, bf16[2560,256]{1,0:T(8,128)(2,1)} %wu_hbm.1, ...), custom_call_target="tpu_custom_call" | custom-call | tf_op jit(solution)/shard_map/moe_layer/pallas_call | solution.py:532
  89.1 2.0 %finish.1 = (bf16[8,2560]{1,0:T(8,128)(2,1)}, bf16[8,2560]{1,0:T(8,128)(2,1)}, f32[8,2560]{1,0:T(8,128)}, f32[160,256]{1,0:T(8,128)}, f32[160,256]{1,0:T(8,128)}, /*index=5*/f32[160,256]{1,0:T(8,128)}) custom-call(f32[3,160,256]{2,1,0:T(8,128)} %get-tuple-element.15.w, f32[2,8,2560]{2,1,0:T(8,128)} %get-tuple-element.16.t, f32[8,2560]{1,0:T(8,128)} %get-tuple-element.17.g), custom_call_target="tpu_custom_call" | custom-call | tf_op jit(solution)/shard_map/finish/pallas_call | solution.py:601
